TPU v7x, 256 devices: a whole 4x4x8 slice. The times are simulated.
256 devices in a mesh: row: 8 (over z_hi, core), col: 32 (over z_lo, y, x).
Axes of the slice: x: 4, y: 4, z: 8 (z_hi: 4, z_lo: 2; z = z_hi * 2 + z_lo), core: 2. Of those that a mesh axis runs over, the one named last changes fastest.
Arguments:
- object_in: float32 [2, 2, 2048, 8192], P(None, None, 'row', 'col'), may hold values from -4 to 4
- probe_in: float32 [2, 256, 256], replicated, may hold values from -5 to 5
- positions: int32 [8, 32, 2, 2], P('row', 'col'), may hold values from -32 to 32
- intensity: float32 [8, 32, 2, 256, 256], P('row', 'col'), may hold values from 0.1 to 8.2
Outputs:
- object_out: float32 [2, 2, 2048, 8192], P(None, None, 'row', 'col')
- probe_out: float32 [2, 256, 256], replicated
Inputs may be any that keep to these rules, and one draw needn't show every extreme that they name: positions[r, c, p] = (dy, dx) places the probe of position p on object rows r * 256 + dy to r * 256 + dy + 255 and columns c * 256 + dx to c * 256 + dx + 255.
All inputs are finite; a program needn't handle non-finite values.
Results may differ from a plain program's by a relative error of at most 0.0003.
Values sent between devices are 32-bit elements; how exact they have to be, the bound alone decides.
A program may use at most 64 MiB of HBM per device.

v0:
```python
import math

import jax
import jax.numpy as jnp
from jax import lax
from jax.sharding import Mesh
from jax.sharding import PartitionSpec as P

RIM = 32
COL = ("col_0", "col_1", "col_2")
ROW = ("row_0", "row_1")
ROW_COL = ("row_0", "row_1", "col_0", "col_1", "col_2")


def passed_along(value, axis, steps):
    count = lax.axis_size(axis)
    initial, last = (max(0, -steps), min(count, count - steps))
    return lax.ppermute(value, axis, [(source, source + steps) for source in range(initial, last)])


def extended(cells, sides, width):
    for axis, dim in sides:
        count = lax.axis_size(axis)
        ends = count - 1
        head = lax.slice_in_dim(cells, 0, width, axis=dim)
        tail = lax.slice_in_dim(cells, cells.shape[dim] - width, cells.shape[dim], axis=dim)
        cells = jnp.concatenate(
            [
                lax.ppermute(tail, axis, [(i, (i + 1) % count) for i in range(ends)]),
                cells,
                lax.ppermute(head, axis, [((i + 1) % count, i) for i in range(ends)]),
            ],
            axis=dim,
        )
    return cells


def by_axis(array, axes):
    for axis in axes:
        array = lax.psum(array, axis)
    return array


def one_axis_at_a_time(array, axes):
    for axis in axes:
        array = lax.pmax(array, axis)
    return array


def tables(extent):
    line_idx = jnp.arange(extent, dtype=jnp.int32)
    turn_count = line_idx[:, None] * line_idx[None, :] % extent
    angles = turn_count.astype(jnp.float32) * (2.0 * math.pi / extent)
    factor = 1.0 / math.sqrt(extent)
    cosine = jnp.cos(angles) * factor
    sine_tab = jnp.sin(angles) * factor
    frequency = ((line_idx + extent // 2) % extent - extent // 2).astype(jnp.float32)
    phases = (
        -math.pi * 8.0 / (extent * extent) * (frequency[:, None] ** 2 + frequency[None, :] ** 2)
    )
    return (cosine, sine_tab, jnp.cos(phases), jnp.sin(phases))


def matrices(cosine, sine_tab, orient):
    return (cosine, sine_tab, float(orient))


def transform(real_part, imag_part, tables_pair):
    cosine, sine_tab, orient = tables_pair
    high = lax.Precision.HIGHEST
    rc = jnp.einsum("byx,xk->byk", real_part, cosine, precision=high)
    rs = jnp.einsum("byx,xk->byk", real_part, sine_tab, precision=high)
    ic = jnp.einsum("byx,xk->byk", imag_part, cosine, precision=high)
    isn = jnp.einsum("byx,xk->byk", imag_part, sine_tab, precision=high)
    mid_re = rc + orient * isn
    mid_im = ic - orient * rs
    out_re = jnp.einsum("ky,byx->bkx", cosine, mid_re, precision=high) + orient * jnp.einsum(
        "ky,byx->bkx", sine_tab, mid_im, precision=high
    )
    out_im = jnp.einsum("ky,byx->bkx", cosine, mid_im, precision=high) - orient * jnp.einsum(
        "ky,byx->bkx", sine_tab, mid_re, precision=high
    )
    return (out_re, out_im)


def times_plain(first_re, first_im, second_re, second_im):
    return (
        first_re * second_re - first_im * second_im,
        first_re * second_im + first_im * second_re,
    )


def times_conj(first_re, first_im, second_re, second_im):
    return (
        first_re * second_re + first_im * second_im,
        first_re * second_im - first_im * second_re,
    )


def tile_gradient(window, probe, offsets, measured, constants):
    cosine, sine_tab, kern_re, kern_im = constants
    forward = matrices(cosine, sine_tab, 1)
    backward = matrices(cosine, sine_tab, -1)
    extent = probe.shape[-1]
    zero_idx = jnp.zeros((), jnp.int32)

    def cut_patch(offset):
        return lax.dynamic_slice(
            window, (zero_idx, zero_idx, offset[0] + RIM, offset[1] + RIM), (2, 2, extent, extent)
        )

    patches = jax.vmap(cut_patch)(offsets)
    first_re, first_im = (patches[:, 0, 0], patches[:, 0, 1])
    second_re, second_im = (patches[:, 1, 0], patches[:, 1, 1])
    probe_re, probe_im = (probe[0], probe[1])
    wave_re, wave_im = times_plain(probe_re, probe_im, first_re, first_im)
    spec_re, spec_im = transform(wave_re, wave_im, forward)
    spec_re, spec_im = times_plain(kern_re, kern_im, spec_re, spec_im)
    prop_re, prop_im = transform(spec_re, spec_im, backward)
    exit_re, exit_im = times_plain(prop_re, prop_im, second_re, second_im)
    far_re, far_im = transform(exit_re, exit_im, forward)
    excess = 2.0 * (far_re * far_re + far_im * far_im - measured)
    back_re, back_im = transform(excess * far_re, excess * far_im, backward)
    grad2_re, grad2_im = times_conj(prop_re, prop_im, back_re, back_im)
    lift_re, lift_im = times_conj(second_re, second_im, back_re, back_im)
    lift_re, lift_im = transform(lift_re, lift_im, forward)
    lift_re, lift_im = times_conj(kern_re, kern_im, lift_re, lift_im)
    enter_re, enter_im = transform(lift_re, lift_im, backward)
    grad1_re, grad1_im = times_conj(probe_re, probe_im, enter_re, enter_im)
    probe_re_g, probe_im_g = times_conj(first_re, first_im, enter_re, enter_im)
    probe_grad = jnp.stack([jnp.sum(probe_re_g, 0), jnp.sum(probe_im_g, 0)], 0)
    pieces = jnp.stack([jnp.stack([grad1_re, grad1_im], 1), jnp.stack([grad2_re, grad2_im], 1)], 1)
    gradient = jnp.zeros(window.shape, jnp.float32)
    for position in range(offsets.shape[0]):
        start_at = (zero_idx, zero_idx, offsets[position, 0] + RIM, offsets[position, 1] + RIM)
        current = lax.dynamic_slice(gradient, start_at, pieces.shape[1:])
        gradient = lax.dynamic_update_slice(gradient, current + pieces[position], start_at)
    return (gradient, probe_grad)


def turned(block):
    return jnp.swapaxes(block, 2, 3)


def cols_then_rows(gradient):
    inner_px = gradient.shape[-1] - 2 * RIM
    upper_end = RIM + inner_px
    from_right = turned(passed_along(turned(gradient[..., :RIM]), COL, -1))
    from_left = turned(passed_along(turned(gradient[..., upper_end:]), COL, 1))
    middle = gradient[..., RIM:upper_end]
    middle = middle.at[..., inner_px - RIM :].add(from_right)
    middle = middle.at[..., :RIM].add(from_left)
    from_below = passed_along(middle[:, :, :RIM, :], ROW, -1)
    from_above = passed_along(middle[:, :, upper_end:, :], ROW, 1)
    interior = middle[:, :, RIM:upper_end, :]
    interior = interior.at[:, :, inner_px - RIM :, :].add(from_below)
    interior = interior.at[:, :, :RIM, :].add(from_above)
    return interior


def local(object_in, probe_in, positions, intensity):
    extent = probe_in.shape[-1]
    constants = tables(extent)
    offsets = positions.reshape(-1, 2)
    measured = intensity.reshape(-1, extent, extent)
    tile_total = lax.axis_size(ROW) * lax.axis_size(COL)
    probe_rate = 2.0 / tile_total
    current = object_in
    window = extended(current, ((ROW, 2), (COL, 3)), RIM)
    gradient, probe_grad = tile_gradient(window, probe_in, offsets, measured, constants)
    probe_total = by_axis(probe_grad, ROW_COL)
    probe_next = probe_in - probe_rate * probe_total
    descent = cols_then_rows(gradient)
    local_peak = jnp.max(descent[:, 0] ** 2 + descent[:, 1] ** 2)
    largest = one_axis_at_a_time(local_peak, ROW_COL)
    current = current - 0.3 * descent / (jnp.sqrt(largest) + 1e-06)
    return (current, probe_next)


def solution(mesh):
    torus = Mesh(mesh.devices.reshape(4, 2, 2, 4, 4), ("row_0", "row_1", "col_0", "col_1", "col_2"))
    placed = (P(None, None, ROW, COL), P(), P(ROW, COL, None, None), P(ROW, COL, None, None, None))
    return jax.shard_map(
        local,
        mesh=torus,
        in_specs=placed,
        out_specs=(P(None, None, ROW, COL), P()),
        check_vma=False,
    )
```

profile of v0, /device:TPU:1, one launch (start us, length us, event | category | flops | bytes accessed | tf_op | source)
XLA Modules:
  0.0 395.7 jit_solution(860421095637435779)
XLA Ops:
  10.1 6.4 %collective-permute-start = (f32[2,2,32,256]{2,3,1,0:T(8,128)}, f32[2,2,32,256]{2,3,1,0:T(8,128)S(1)}, u32[]{:S(2)}, u32[]{:S(2)}) collective-permute-start(f32[2,2,32,256]{2,3,1,0:T(8,128)} %get-tuple-element.96), channel_id=1, source_target_pairs={{0,32},{32,64},{64,96},{96,128},{128,160},{160,192},{192,224},{1,3... | collective-permute-start | bytes 393224 | tf_op jit(solution)/shard_map/ppermute | solution.py:29
  16.5 1.9 collective-permute-start.1
  21.3 2.1 copy.98
  23.4 10.3 %collective-permute-done.1 = f32[2,2,32,256]{2,3,1,0:T(8,128)S(1)} collective-permute-done((f32[2,2,32,256]{2,3,1,0:T(8,128)}, f32[2,2,32,256]{2,3,1,0:T(8,128)S(1)}, u32[]{:S(2)}, u32[]{:S(2)}) %collective-permute-start.1) | collective-permute-done | bytes 131104 | tf_op jit(solution)/shard_map/ppermute | solution.py:31
  34.0 3.1 collective-permute-start.2
  39.7 3.8 collective-permute-done.3
  45.3 11.2 %while.5 = (s32[]{:T(128)}, f32[2,2,320,320]{2,3,1,0:T(8,128)S(1)}, s32[2,4]{1,0:T(2,128)S(1)}, f32[2,2,2,256,256]{3,4,0,2,1:T(8,128)}, s32[]{:T(128)}) while((s32[]{:T(128)}, f32[2,2,320,320]{2,3,1,0:T(8,128)S(1)}, s32[2,4]{1,0:T(2,128)S(1)}, f32[2,2,2,256,256]{3,4,0,2,1:T(8,128)}, s32[]{:T(128)}) %tuple.62), condition=%wide.while_cond.4, body=%wide.while_body.4.sunk | while | flops 2 | bytes 21496496 | solution.py:108
  56.5 3.4 fusion.112
  59.9 3.2 fusion.116
  63.1 1.9 convolution_subtract_fusion.5
  66.9 1.9 convolution_add_fusion.5
  70.6 2.3 fusion.22
  74.7 1.9 fusion.108
  76.6 1.9 fusion.104
  78.5 1.9 fusion.21
  82.2 2.1 fusion.20
  87.9 1.9 fusion.32
  93.5 2.1 convolution_add_fusion.3
  104.7 1.9 fusion.92
  106.7 2.3 fusion.88
  109.0 1.9 fusion.13
  110.9 1.9 fusion.12
  118.4 2.1 add_bitcast_fusion
  129.8 2.1 fusion.82
  135.6 1.9 fusion.76
  137.4 1.9 fusion.72
  139.3 1.9 fusion.5
  141.2 2.3 fusion.4
  149.0 2.0 fusion.38
  158.7 52.4 %all-reduce.6.cloned.1.call-done = f32[2,256,256]{1,2,0:T(8,128)} async-done(((f32[2,256,256]{1,2,0:T(8,128)}), f32[2,256,256]{1,2,0:T(8,128)}) %all-reduce.6.cloned.1.call-update) | async-done | bytes 524304 | tf_op jit(solution)/shard_map/psum | solution.py:40
  211.2 2.1 fusion.25
  213.4 13.5 %dynamic_update_slice.6 = f32[2,2,320,320]{2,3,1,0:T(8,128)S(1)} dynamic-update-slice(f32[2,2,320,320]{2,3,1,0:T(8,128)S(1)} %broadcast_in_dim.2, f32[2,2,256,256]{2,3,1,0:T(8,128)} %fusion.25, s32[]{:T(128)} %constant.162.clone.1, s32[]{:T(128)} %constant.162.clone.1, s32[]{:T(128)S(6)} %select_n.155, s32[]{:T(128)S(6)} %select_n.156) | dynamic-update-slice | bytes 2097156 | tf_op jit(solution)/shard_map/dynamic_update_slice | solution.py:137
  226.9 2.4 fusion.27
  229.3 13.8 %dynamic_update_slice.7 = f32[2,2,320,320]{2,3,1,0:T(8,128)S(1)} dynamic-update-slice(f32[2,2,320,320]{2,3,1,0:T(8,128)S(1)} %dynamic_update_slice.6, f32[2,2,256,256]{2,3,1,0:T(8,128)} %fusion.27, s32[]{:T(128)} %constant.162.clone.1, s32[]{:T(128)} %constant.162.clone.1, s32[]{:T(128)S(6)} %select_n.157, s32[]{:T(128)S(6)} %select_n.158) | dynamic-update-slice | bytes 2097156 | tf_op jit(solution)/shard_map/dynamic_update_slice | solution.py:137
  246.2 4.0 %collective-permute-start.5 = (f32[2,2,32,320]{3,2,1,0:T(8,128)S(1)}, f32[2,2,32,320]{3,2,1,0:T(8,128)S(1)}, u32[]{:S(2)}, u32[]{:S(2)}) collective-permute-start(f32[2,2,32,320]{3,2,1,0:T(8,128)S(1)} %copy-done.13), channel_id=1, source_target_pairs={{0,1},{1,2},{2,3},{3,4},{4,5},{5,6},{6,7},{7,8},{8,9},{9,10},{10,1... | collective-permute-start | bytes 491528 | tf_op jit(solution)/shard_map/ppermute | solution.py:18
  252.9 34.3 %all-reduce.10.cloned.1.call-done = f32[2,256,256]{1,2,0:T(8,128)} async-done(((f32[2,256,256]{1,2,0:T(8,128)}), f32[2,256,256]{1,2,0:T(8,128)}) %all-reduce.10.cloned.1.call-update) | async-done | bytes 524304 | tf_op jit(solution)/shard_map/psum | solution.py:40
  288.3 2.7 collective-permute-start.6
  291.3 4.1 %collective-permute-start.7 = (f32[2,2,32,256]{2,3,1,0:T(8,128)}, f32[2,2,32,256]{2,3,1,0:T(8,128)}, u32[]{:S(2)}, u32[]{:S(2)}) collective-permute-start(f32[2,2,32,256]{2,3,1,0:T(8,128)} %get-tuple-element.88), channel_id=1, source_target_pairs={{0,32},{32,64},{64,96},{96,128},{128,160},{160,192},{192,224},{1,3... | collective-permute-start | bytes 393224 | tf_op jit(solution)/shard_map/ppermute | solution.py:18
  295.4 10.1 %collective-permute-done.6 = f32[2,2,32,256]{2,3,1,0:T(8,128)S(1)} collective-permute-done((f32[2,2,32,256]{2,3,1,0:T(8,128)S(1)}, f32[2,2,32,256]{2,3,1,0:T(8,128)S(1)}, u32[]{:S(2)}, u32[]{:S(2)}) %collective-permute-start.6) | collective-permute-done | bytes 131104 | tf_op jit(solution)/shard_map/ppermute | solution.py:18
  305.6 2.6 scatter-add.16
  308.2 27.7 %all-reduce.12.cloned.1.call-done = f32[2,256,256]{1,2,0:T(8,128)} async-done(((f32[2,256,256]{1,2,0:T(8,128)}), f32[2,256,256]{1,2,0:T(8,128)}) %all-reduce.12.cloned.1.call-update) | async-done | bytes 524304 | tf_op jit(solution)/shard_map/psum | solution.py:40
  337.1 2.3 scatter-add.19
  340.1 11.3 %pmax.35 = f32[]{:T(128)} all-reduce(f32[]{:T(128)} %fusion.29), channel_id=1, replica_groups=mesh['row_0'=4,'row_1'=2,'col_0'=2,'col_1'=4,'col_2'=4] {'row_0'}, use_global_device_ids=true, to_apply=%region_1.2 | all-reduce | flops 1 | bytes 8 | tf_op jit(solution)/shard_map/pmax | solution.py:46
  351.4 7.6 %pmax.36 = f32[]{:T(128)} all-reduce(f32[]{:T(128)} %pmax.35), channel_id=1, replica_groups=mesh['row_0'=4,'row_1'=2,'col_0'=2,'col_1'=4,'col_2'=4] {'row_1'}, use_global_device_ids=true, to_apply=%region_2.3 | all-reduce | flops 1 | bytes 8 | tf_op jit(solution)/shard_map/pmax | solution.py:46
  359.1 4.8 %pmax.37 = f32[]{:T(128)} all-reduce(f32[]{:T(128)} %pmax.36), channel_id=1, replica_groups=mesh['row_0'=4,'row_1'=2,'col_0'=2,'col_1'=4,'col_2'=4] {'col_0'}, use_global_device_ids=true, to_apply=%region_3.4 | all-reduce | flops 1 | bytes 8 | tf_op jit(solution)/shard_map/pmax | solution.py:46
  363.8 8.1 %pmax.38 = f32[]{:T(128)} all-reduce(f32[]{:T(128)} %pmax.37), channel_id=1, replica_groups=mesh['row_0'=4,'row_1'=2,'col_0'=2,'col_1'=4,'col_2'=4] {'col_1'}, use_global_device_ids=true, to_apply=%region_4.5 | all-reduce | flops 1 | bytes 8 | tf_op jit(solution)/shard_map/pmax | solution.py:46
  372.9 8.8 %pmax.39 = f32[]{:T(128)} all-reduce(f32[]{:T(128)} %pmax.38), channel_id=1, replica_groups=mesh['row_0'=4,'row_1'=2,'col_0'=2,'col_1'=4,'col_2'=4] {'col_2'}, use_global_device_ids=true, to_apply=%region_5.6 | all-reduce | flops 1 | bytes 8 | tf_op jit(solution)/shard_map/pmax | solution.py:46
  383.9 3.0 all-reduce.14.cloned.1.call-done
  (123 shorter events, 85.1 us)
Async XLA Ops:
  7.2 11.3 %copy-start.11 = (f32[2,256,256]{2,1,0:T(8,128)S(1)}, f32[2,256,256]{2,1,0:T(8,128)}, u32[]{:S(2)}) copy-start(f32[2,256,256]{2,1,0:T(8,128)} %param.13) | copy-start | bytes 1572868
  7.2 203.9 %all-reduce.6.cloned.1.call-start = ((), (), s32[]{:S(2)}) async-start(), calls=%async_computation | async-start | bytes 1048576 | tf_op jit(solution)/shard_map/psum | solution.py:40
  8.8 34.7 %copy-start.2 = (f32[2,2,256,256]{2,3,1,0:T(8,128)}, f32[2,2,256,256]{2,3,1,0:T(8,128)S(1)}, u32[]{:S(2)}) copy-start(f32[2,2,256,256]{2,3,1,0:T(8,128)S(1)} %copy.124) | copy-start | bytes 3145732
  10.1 13.2 %copy-start.14 = (s32[1,1,2,2]{3,2,1,0:T(2,128)S(1)}, s32[1,1,2,2]{3,2,1,0:T(2,128)}, u32[]{:S(2)}) copy-start(s32[1,1,2,2]{3,2,1,0:T(2,128)} %param.14) | copy-start | bytes 52
  10.1 13.3 %collective-permute-start = (f32[2,2,32,256]{2,3,1,0:T(8,128)}, f32[2,2,32,256]{2,3,1,0:T(8,128)S(1)}, u32[]{:S(2)}, u32[]{:S(2)}) collective-permute-start(f32[2,2,32,256]{2,3,1,0:T(8,128)} %get-tuple-element.96), channel_id=1, source_target_pairs={{0,32},{32,64},{64,96},{96,128},{128,160},{160,192},{192,224},{1,3... | collective-permute-start | bytes 393224 | tf_op jit(solution)/shard_map/ppermute | solution.py:29
  16.5 17.2 %collective-permute-start.1 = (f32[2,2,32,256]{2,3,1,0:T(8,128)}, f32[2,2,32,256]{2,3,1,0:T(8,128)S(1)}, u32[]{:S(2)}, u32[]{:S(2)}) collective-permute-start(f32[2,2,32,256]{2,3,1,0:T(8,128)} %get-tuple-element.97), channel_id=1, source_target_pairs={{32,0},{64,32},{96,64},{128,96},{160,128},{192,160},{224,192},{33,... | collective-permute-start | bytes 393224 | tf_op jit(solution)/shard_map/ppermute | solution.py:31
  23.4 16.3 %copy-start.8 = (f32[2,2,32,256]{2,3,1,0:T(8,128)}, f32[2,2,32,256]{2,3,1,0:T(8,128)S(1)}, u32[]{:S(2)}) copy-start(f32[2,2,32,256]{2,3,1,0:T(8,128)S(1)} %collective-permute-done) | copy-start | bytes 393220
  33.8 5.9 %copy-start.9 = (f32[2,2,32,256]{2,3,1,0:T(8,128)}, f32[2,2,32,256]{2,3,1,0:T(8,128)S(1)}, u32[]{:S(2)}) copy-start(f32[2,2,32,256]{2,3,1,0:T(8,128)S(1)} %collective-permute-done.1) | copy-start | bytes 393220
  34.0 5.7 %collective-permute-start.2 = (f32[2,2,320,32]{2,3,1,0:T(8,128)S(1)}, f32[2,2,320,32]{2,3,1,0:T(8,128)S(1)}, u32[]{:S(2)}, u32[]{:S(2)}) collective-permute-start(f32[2,2,320,32]{2,3,1,0:T(8,128)S(1)} %get-tuple-element.84), channel_id=1, source_target_pairs={{0,1},{1,2},{2,3},{3,4},{4,5},{5,6},{6,7},{7,8},{8,9},{9,10},{10,1... | collective-permute-start | bytes 491528 | tf_op jit(solution)/shard_map/ppermute | solution.py:29
  37.1 6.4 %collective-permute-start.3 = (f32[2,2,320,32]{2,3,1,0:T(8,128)S(1)}, f32[2,2,320,32]{2,3,1,0:T(8,128)S(1)}, u32[]{:S(2)}, u32[]{:S(2)}) collective-permute-start(f32[2,2,320,32]{2,3,1,0:T(8,128)S(1)} %get-tuple-element.85), channel_id=1, source_target_pairs={{1,0},{2,1},{3,2},{4,3},{5,4},{6,5},{7,6},{8,7},{9,8},{10,9},{11,1... | collective-permute-start | bytes 491528 | tf_op jit(solution)/shard_map/ppermute | solution.py:31
  45.3 1.3 copy-start
  48.8 1.9 copy-start.1
  50.8 1.3 copy-start
  54.3 1.9 copy-start.1
  56.5 6.6 %copy-start.5 = (f32[256,256]{0,1:T(8,128)S(1)}, f32[256,256]{0,1:T(8,128)}, u32[]{:S(2)}) copy-start(f32[256,256]{0,1:T(8,128)} %copy.64) | copy-start | bytes 786436
  56.5 6.6 %copy-start.6 = (f32[256,256]{0,1:T(8,128)S(1)}, f32[256,256]{0,1:T(8,128)}, u32[]{:S(2)}) copy-start(f32[256,256]{0,1:T(8,128)} %copy.71) | copy-start | bytes 786436
  56.5 6.6 %copy-start.7 = (f32[2,2,2,256,256]{3,4,0,2,1:T(8,128)S(1)}, f32[2,2,2,256,256]{3,4,0,2,1:T(8,128)}, u32[]{:S(2)}) copy-start(f32[2,2,2,256,256]{3,4,0,2,1:T(8,128)} %get-tuple-element.57) | copy-start | bytes 6291460
  99.2 5.5 %copy-start.4 = (f32[1,1,2,256,256]{3,4,2,1,0:T(8,128)S(1)}, f32[1,1,2,256,256]{3,4,2,1,0:T(8,128)}, u32[]{:S(2)}) copy-start(f32[1,1,2,256,256]{3,4,2,1,0:T(8,128)} %copy.98) | copy-start | bytes 1572868
  151.9 93.4 %all-reduce.8.cloned.1.call-start = ((), (), s32[]{:S(2)}) async-start(), calls=%async_computation.1 | async-start | bytes 1048576 | tf_op jit(solution)/shard_map/psum | solution.py:40
  211.1 76.1 %all-reduce.10.cloned.1.call-start = ((), (), s32[]{:S(2)}) async-start(), calls=%async_computation.2 | async-start | bytes 1048576 | tf_op jit(solution)/shard_map/psum | solution.py:40
  243.9 6.7 %collective-permute-start.4 = (f32[2,2,32,320]{3,2,1,0:T(8,128)}, f32[2,2,32,320]{3,2,1,0:T(8,128)}, u32[]{:S(2)}, u32[]{:S(2)}) collective-permute-start(f32[2,2,32,320]{3,2,1,0:T(8,128)} %get-tuple-element.87), channel_id=1, source_target_pairs={{1,0},{2,1},{3,2},{4,3},{5,4},{6,5},{7,6},{8,7},{9,8},{10,9},{11,1... | collective-permute-start | bytes 491528 | tf_op jit(solution)/shard_map/ppermute | solution.py:18
  245.3 90.6 %all-reduce.12.cloned.1.call-start = ((), (), s32[]{:S(2)}) async-start(), calls=%async_computation.3 | async-start | bytes 1048576 | tf_op jit(solution)/shard_map/psum | solution.py:40
  245.3 0.9 copy-start.13
  246.2 6.6 %collective-permute-start.5 = (f32[2,2,32,320]{3,2,1,0:T(8,128)S(1)}, f32[2,2,32,320]{3,2,1,0:T(8,128)S(1)}, u32[]{:S(2)}, u32[]{:S(2)}) collective-permute-start(f32[2,2,32,320]{3,2,1,0:T(8,128)S(1)} %copy-done.13), channel_id=1, source_target_pairs={{0,1},{1,2},{2,3},{3,4},{4,5},{5,6},{6,7},{7,8},{8,9},{9,10},{10,1... | collective-permute-start | bytes 491528 | tf_op jit(solution)/shard_map/ppermute | solution.py:18
  287.2 99.7 %all-reduce.14.cloned.1.call-start = ((), (), s32[]{:S(2)}) async-start(), calls=%async_computation.4 | async-start | bytes 1048576 | tf_op jit(solution)/shard_map/psum | solution.py:40
  288.3 17.3 %collective-permute-start.6 = (f32[2,2,32,256]{2,3,1,0:T(8,128)S(1)}, f32[2,2,32,256]{2,3,1,0:T(8,128)S(1)}, u32[]{:S(2)}, u32[]{:S(2)}) collective-permute-start(f32[2,2,32,256]{2,3,1,0:T(8,128)S(1)} %get-tuple-element.89), channel_id=1, source_target_pairs={{32,0},{64,32},{96,64},{128,96},{160,128},{192,160},{224,192},{33,... | collective-permute-start | bytes 393224 | tf_op jit(solution)/shard_map/ppermute | solution.py:18
  291.3 44.6 %collective-permute-start.7 = (f32[2,2,32,256]{2,3,1,0:T(8,128)}, f32[2,2,32,256]{2,3,1,0:T(8,128)}, u32[]{:S(2)}, u32[]{:S(2)}) collective-permute-start(f32[2,2,32,256]{2,3,1,0:T(8,128)} %get-tuple-element.88), channel_id=1, source_target_pairs={{0,32},{32,64},{64,96},{96,128},{128,160},{160,192},{192,224},{1,3... | collective-permute-start | bytes 393224 | tf_op jit(solution)/shard_map/ppermute | solution.py:18
  335.9 36.0 %copy-start.12 = (f32[2,256,256]{2,1,0:T(8,128)S(1)}, f32[2,256,256]{2,1,0:T(8,128)}, u32[]{:S(2)}) copy-start(f32[2,256,256]{2,1,0:T(8,128)} %param.13) | copy-start | bytes 1572868
  337.1 45.4 %copy-start.3 = (f32[2,2,256,256]{2,3,1,0:T(8,128)S(1)}, f32[2,2,256,256]{2,3,1,0:T(8,128)}, u32[]{:S(2)}) copy-start(f32[2,2,256,256]{2,3,1,0:T(8,128)} %copy-done.2) | copy-start | bytes 3145732
  382.6 4.3 %copy-start.10 = (f32[2,256,256]{1,2,0:T(8,128)S(1)}, f32[2,256,256]{1,2,0:T(8,128)}, u32[]{:S(2)}) copy-start(f32[2,256,256]{1,2,0:T(8,128)} %copy.125) | copy-start | bytes 1572868
Sparse Core Ops, SparseCore 0:
  152.0 59.0 all-reduce.5
  213.7 30.4 all-reduce.7
  246.8 40.3 all-reduce.9
  289.4 46.4 all-reduce.11
  338.1 48.8 all-reduce.13
where the time goes:
time: 402 us; the launch traced here: 396 us
  waiting for transfers between devices  145 us (36%)
  matrix products  94.1 us (23%)
  local copies, waits for them, and re-layouts  56.8 us (14%)
  blocking collectives  40.6 us (10%)
  starting transfers between devices  25 us (6%)
  between operations  20.4 us (5%)
  other arithmetic  13.9 us (3%)
    psum x5, waiting for transfers between devices, by_axis(): array = lax.psum(array, axis)  117 us
    pmax x5, blocking collectives, one_axis_at_a_time(): array = lax.pmax(array, axis)  40.6 us
    dynamic_update_slice x2, local copies, waits for them, and re-layouts, tile_gradient(): lax.dynamic_update_slice(gradient, current + pieces[position], start_at)  27.3 us
    ppermute x2, waiting for transfers between devices, extended(): lax.ppermute(head, axis, [((i + 1) % count, i) for i in range(ends)])  14.2 us
    dot_general x6, matrix products, transform(): ic = jnp.einsum('byx,xk->byk', imag_part, cosine, precision=high)  13.1 us
    dot_general x6, matrix products, transform(): rc = jnp.einsum('byx,xk->byk', real_part, cosine, precision=high)  12.6 us
    ppermute x4, starting transfers between devices, passed_along(): lax.ppermute(value, axis, [(source, source + steps) for source in range(i...  12.1 us
    dot_general x6, matrix products, transform(): rs = jnp.einsum('byx,xk->byk', real_part, sine_tab, precision=high)  11.8 us
  transfers between devices with their start and end apart: 13, of which 10 were waited for; matrix products, arithmetic and copies ran while one was open for 13% of the time, Pallas kernels for 0%

commit v1 on v0

v1 whole, which is shorter than its diff:
```python
import functools
import math

import jax
import jax.numpy as jnp
import numpy as np
from jax import lax
from jax.experimental import pallas as pl
from jax.experimental.pallas import tpu as pltpu
from jax.sharding import PartitionSpec as P

RIM = 32
MESH = pl.DeviceIdType.MESH
VMEM = pltpu.VMEM
AROUND = ((-1, 0), (1, 0), (0, -1), (0, 1), (-1, -1), (-1, 1), (1, -1), (1, 1))
CORES = 2
NYX = (4, 4)


def split_of(matrix):
    high = matrix.astype(jnp.bfloat16)
    low = (matrix - high.astype(np.float64)).astype(jnp.bfloat16)
    return np.stack([np.asarray(high), np.asarray(low)])


def stacked(weight):
    real, imag = weight.real, weight.imag
    return np.block([[real, imag], [-imag, real]])


def weights(extent):
    half = extent // 2
    idx = np.arange(extent)
    freq = ((idx + half) % extent - half).astype(np.float64)
    turn = np.exp(-2j * np.pi * ((idx[:, None] * idx[None, :]) % extent) / extent)
    phase = np.exp(-8j * np.pi * freq**2 / extent**2)
    band = (np.conj(turn) * phase[None, :]) @ turn / extent
    left, right = band[:half, :half], band[:half, half:]
    even = turn[:half, 0::2] / math.sqrt(extent)
    odd = turn[:half, 1::2] / math.sqrt(extent)
    plus, minus = stacked((left + right) / 2), stacked((left - right) / 2)
    ev, od = stacked(even), stacked(odd)
    table = np.stack([split_of(m) for m in (plus, minus, ev, od, od.T)])
    order = np.concatenate([idx[0::2], idx[1::2]])
    perm = np.zeros((extent, extent), np.float32)
    perm[order, idx] = 1.0
    return table, perm.astype(jnp.bfloat16)


def parts(x):
    high = x.astype(jnp.bfloat16)
    return high, (x - high.astype(jnp.float32)).astype(jnp.bfloat16)


def dot(a, b):
    return jnp.dot(a, b, preferred_element_type=jnp.float32)


def times_right(x, w_ref, k):
    high, low = parts(x)
    wh, wl = w_ref[k, 0], w_ref[k, 1]
    return dot(jnp.concatenate([high, low, high], 1), jnp.concatenate([wh, wh, wl], 0))


def times_left(x, w_ref, k):
    high, low = parts(x)
    wh, wl = w_ref[k, 0], w_ref[k, 1]
    return dot(jnp.concatenate([wh, wh, wl], 1), jnp.concatenate([high, low, high], 0))


def fold(x):
    h = x.shape[0] // 2
    s, d = x[:h] + x[h:], x[:h] - x[h:]
    return [[s[:, :h] + s[:, h:], s[:, :h] - s[:, h:]], [d[:, :h] + d[:, h:], d[:, :h] - d[:, h:]]]


def unfold(b):
    top_s, top_d = b[0][0] + b[0][1], b[0][0] - b[0][1]
    bot_s, bot_d = b[1][0] + b[1][1], b[1][0] - b[1][1]
    s = jnp.concatenate([top_s, top_d], 1)
    d = jnp.concatenate([bot_s, bot_d], 1)
    return jnp.concatenate([s + d, s - d], 0)


def sandwich(re, im, w_ref, right, left):
    h = re[0][0].shape[0]
    out = [None, None]
    for j in (0, 1):
        k, swap = right[j]
        first, second = (im, re) if swap else (re, im)
        x = jnp.concatenate(
            [jnp.concatenate([first[i][j], second[i][j]], 1) for i in (0, 1)], 0
        )
        y = times_right(x, w_ref, k)
        a, b = y[:, :h], y[:, h:]
        out[j] = (b, a) if swap else (a, b)
    res_re, res_im = [None, None], [None, None]
    for i in (0, 1):
        k, swap = left[i]
        rows = slice(i * h, (i + 1) * h)
        r = jnp.concatenate([out[0][0][rows], out[1][0][rows]], 1)
        m = jnp.concatenate([out[0][1][rows], out[1][1][rows]], 1)
        y = times_left(jnp.concatenate([m, r] if swap else [r, m], 0), w_ref, k)
        a, b = y[:h], y[h:]
        r, m = (b, a) if swap else (a, b)
        res_re[i] = [r[:, :h], r[:, h:]]
        res_im[i] = [m[:, :h], m[:, h:]]
    return res_re, res_im


PROP = (((0, False), (1, False)), ((0, True), (1, True)))
PROP_CONJ = (((0, True), (1, True)), ((0, False), (1, False)))
FORWARD = (((2, False), (3, False)), ((2, True), (4, False)))
BACKWARD = (((2, True), (4, False)), ((2, False), (3, False)))


def tile_kernel(
    pos_ref, obj_ref, top_ref, bottom_ref, left_ref, right_ref, probe_ref, meas_ref, w_ref, perm_ref,
    core_ref, gt_ref, gb_ref, gl_ref, gr_ref, gp_ref,
    win, cut, mid, pad, seen,
):
    n = probe_ref.shape[-1]
    h = n // 2
    npos = cut.shape[0]
    lane = lax.broadcasted_iota(jnp.int32, (8, 128), 1)

    for q in range(4):
        for t in (0, 1):
            cols = slice(128 * t, 128 * t + 128)
            win[q, t + 1, RIM : RIM + n, :] = obj_ref[q, :, cols]
            win[q, t + 1, :RIM, :] = top_ref[q, :, cols]
            win[q, t + 1, RIM + n :, :] = bottom_ref[q, :, cols]
        win[q, 0] = pltpu.roll(left_ref[...], (96 - 32 * q) % 128, 1)
        win[q, 3] = pltpu.roll(right_ref[...], (128 - 32 * q) % 128, 1) if q else right_ref[...]
    zeros = jnp.zeros((64, 128), jnp.float32)
    for p in range(npos):
        for q in range(4):
            for t in (0, 1):
                pad[p, q, t, 0:64, :] = zeros
                pad[p, q, t, 64 + n :, :] = zeros

    def keep(p, q, value):
        pad[p, q, 0, 64 : 64 + n, :] = value[:, :128]
        pad[p, q, 1, 64 : 64 + n, :] = value[:, 128:]

    offs = [(pos_ref[2 * p], pos_ref[2 * p + 1]) for p in range(npos)]

    def cut_rows(i, carry):
        at = pl.multiple_of(i * 8, 8)
        for p in range(npos):
            dy, dx = offs[p]
            shift = lax.rem(128 - dx, 128)
            high, low = lane >= 128 - dx, lane < -dx
            for q in range(4):
                rows = pl.ds(RIM + dy + i * 8, 8)
                r = [pltpu.roll(win[q, t, rows, :], shift, 1) for t in range(4)]
                for t in (1, 2):
                    cut[p, q, pl.ds(at, 8), 128 * (t - 1) : 128 * t] = jnp.where(
                        high, r[t + 1], jnp.where(low, r[t - 1], r[t])
                    )
        return carry

    lax.fori_loop(0, n // 8, cut_rows, 0)

    for p in range(npos):
        pr, pi = probe_ref[0], probe_ref[1]
        ar, ai = cut[p, 0], cut[p, 1]
        re, im = sandwich(fold(pr * ar - pi * ai), fold(pr * ai + pi * ar), w_ref, *PROP)
        qr, qi = unfold(re), unfold(im)
        mid[p, 0], mid[p, 1] = qr, qi
        br, bi = cut[p, 2], cut[p, 3]
        re, im = sandwich(fold(qr * br - qi * bi), fold(qr * bi + qi * br), w_ref, *FORWARD)
        for t in (0, 1):
            seen[p, t] = meas_ref[p, :, 128 * t : 128 * t + 128]
        meas = jnp.concatenate(
            [
                jnp.concatenate([seen[p, t, pl.ds(i, h, stride=2), :] for t in (0, 1)], 1)
                for i in (0, 1)
            ],
            0,
        )
        mh, ml = parts(meas)
        meas = dot(jnp.concatenate([mh, ml], 1), jnp.concatenate([perm_ref[...], perm_ref[...]], 0))
        for i in (0, 1):
            for j in (0, 1):
                fr, fi = re[i][j], im[i][j]
                ex = 2.0 * (fr * fr + fi * fi - meas[i * h : (i + 1) * h, j * h : (j + 1) * h])
                re[i][j], im[i][j] = ex * fr, ex * fi
        re, im = sandwich(re, im, w_ref, *BACKWARD)
        hr, hi = unfold(re), unfold(im)
        qr, qi = mid[p, 0], mid[p, 1]
        keep(p, 2, qr * hr + qi * hi)
        keep(p, 3, qr * hi - qi * hr)
        br, bi = cut[p, 2], cut[p, 3]
        re, im = sandwich(fold(br * hr + bi * hi), fold(br * hi - bi * hr), w_ref, *PROP_CONJ)
        er, ei = unfold(re), unfold(im)
        pr, pi = probe_ref[0], probe_ref[1]
        keep(p, 0, pr * er + pi * ei)
        keep(p, 1, pr * ei - pi * er)
        ar, ai = cut[p, 0], cut[p, 1]
        if p == 0:
            gp_ref[0] = ar * er + ai * ei
            gp_ref[1] = ar * ei - ai * er
        else:
            gp_ref[0] += ar * er + ai * ei
            gp_ref[1] += ar * ei - ai * er

    quarter = lax.div(lane, 32)

    def place(i, mid_ref, first):
        at = pl.multiple_of((i - first) * 8, 8)
        left = right = None
        for q in range(4):
            sums = None
            for p in range(npos):
                dy, dx = offs[p]
                shift = lax.rem(128 + dx, 128)
                low, high = lane < dx, lane >= 128 + dx
                rows = pl.ds(RIM - dy + i * 8, 8)
                a, b = (pltpu.roll(pad[p, q, t, rows, :], shift, 1) for t in (0, 1))
                o = jnp.zeros_like(a)
                got = [
                    jnp.where(high, a, o),
                    jnp.where(low, o, jnp.where(high, b, a)),
                    jnp.where(low, a, jnp.where(high, o, b)),
                    jnp.where(low, b, o),
                ]
                sums = got if sums is None else [u + v for u, v in zip(sums, got)]
            mid_ref[q, pl.ds(at, 8), 0:128] = sums[1]
            mid_ref[q, pl.ds(at, 8), 128:256] = sums[2]
            lft = pltpu.roll(sums[0], (32 * q + 32) % 128, 1)
            rgt = pltpu.roll(sums[3], 32 * q, 1) if q else sums[3]
            left = lft if left is None else jnp.where(quarter == q, lft, left)
            right = rgt if right is None else jnp.where(quarter == q, rgt, right)
        row = pl.multiple_of(i * 8, 8)
        gl_ref[pl.ds(row, 8), :] = left
        gr_ref[pl.ds(row, 8), :] = right

    k = RIM // 8

    def loop(lo, hi, ref):
        def step(i, carry):
            place(i, ref, lo)
            return carry

        lax.fori_loop(lo, hi, step, 0)

    loop(0, k, gt_ref)
    loop(k, k + n // 8, core_ref)
    loop(k + n // 8, 2 * k + n // 8, gb_ref)


def place_of():
    return lax.axis_index("row"), lax.axis_index("col")


def neighbours(rows, cols):
    r, c = place_of()
    out = []
    for dr, dc in AROUND:
        ok = None
        if dr:
            ok = r > 0 if dr < 0 else r < rows - 1
        if dc:
            side = c > 0 if dc < 0 else c < cols - 1
            ok = side if ok is None else jnp.logical_and(ok, side)
        out.append((ok, (r + dr, c + dc)))
    return out


def opposite(d):
    dr, dc = AROUND[d]
    return AROUND.index((-dr, -dc))


def greet(rows, cols, extra=()):
    barrier = pltpu.get_barrier_semaphore()
    r, c = place_of()
    for ok, where in neighbours(rows, cols):

        @pl.when(ok)
        def _(where=where):
            pl.semaphore_signal(barrier, inc=1, device_id=where, device_id_type=MESH)

    for where in extra:
        pl.semaphore_signal(barrier, inc=1, device_id=where, device_id_type=MESH)
    tall = 1 + jnp.where(r > 0, 1, 0) + jnp.where(r < rows - 1, 1, 0)
    wide = 1 + jnp.where(c > 0, 1, 0) + jnp.where(c < cols - 1, 1, 0)
    pl.semaphore_wait(barrier, tall * wide - 1 + len(extra))


def swap_rims(rows, cols, sources, targets, send_sem, recv_sem):
    for d, (ok, where) in enumerate(neighbours(rows, cols)):
        copy = pltpu.make_async_remote_copy(
            src_ref=sources[d],
            dst_ref=targets[opposite(d)],
            send_sem=send_sem.at[d],
            recv_sem=recv_sem.at[opposite(d)],
            device_id=where,
            device_id_type=MESH,
        )
        pl.when(ok)(copy.start)
        target = targets[d]

        @pl.when(jnp.logical_not(ok))
        def _(target=target):
            target[...] = jnp.zeros(target.shape, target.dtype)


def finish_rims(rows, cols, sources, targets, send_sem, recv_sem):
    for d, (ok, where) in enumerate(neighbours(rows, cols)):
        sent = pltpu.make_async_remote_copy(
            src_ref=sources[d],
            dst_ref=targets[d],
            send_sem=send_sem.at[d],
            recv_sem=recv_sem.at[d],
            device_id=where,
            device_id_type=MESH,
        )
        pl.when(ok)(sent.wait)


def halo_kernel(rows, cols, obj_ref, top_ref, bottom_ref, left_ref, right_ref, pl_buf, pr_buf, send_sem, recv_sem):
    n = obj_ref.shape[-1]
    lane = lax.broadcasted_iota(jnp.int32, (n, 128), 1)
    quarter = lax.div(lane, 32)
    left = obj_ref[0, :, 0:128]
    right = pltpu.roll(obj_ref[0, :, n - 128 :], 32, 1)
    for q in range(1, 4):
        left = jnp.where(quarter == q, pltpu.roll(obj_ref[q, :, 0:128], 32 * q, 1), left)
        right = jnp.where(
            quarter == q, pltpu.roll(obj_ref[q, :, n - 128 :], (32 * q + 32) % 128, 1), right
        )
    pl_buf[...] = left
    pr_buf[...] = right
    greet(rows, cols)
    lo, hi = pl.ds(0, RIM), pl.ds(n - RIM, RIM)
    sources = [
        obj_ref.at[:, lo, :], obj_ref.at[:, hi, :], pl_buf, pr_buf,
        pl_buf.at[lo, :], pr_buf.at[lo, :], pl_buf.at[hi, :], pr_buf.at[hi, :],
    ]
    first, core, last = pl.ds(0, RIM), pl.ds(RIM, n), pl.ds(RIM + n, RIM)
    targets = [
        top_ref, bottom_ref, left_ref.at[core, :], right_ref.at[core, :],
        left_ref.at[first, :], right_ref.at[first, :], left_ref.at[last, :], right_ref.at[last, :],
    ]
    swap_rims(rows, cols, sources, targets, send_sem, recv_sem)
    finish_rims(rows, cols, sources, targets, send_sem, recv_sem)


def sum_kernel(
    rows, cols, nyx,
    gp_ref, core_ref, gt_ref, gb_ref, gl_ref, gr_ref,
    total_ref, descent_ref, peak_ref,
    theirs, ours, slots, zslots, mine, zpeak, xpeak, ppeak,
    rt, rb, rl, rr, corners,
    send_rim, recv_rim, send_pair, recv_pair, send_xy, recv_xy, send_z, recv_z,
    send_zm, recv_zm, send_xm, recv_xm, send_all, recv_all, send_back, recv_back, send_pm, recv_pm,
):
    n = gp_ref.shape[-1]
    ny, nx = nyx
    nxy = ny * nx
    nzl = cols // nxy
    nz = nzl * (rows // CORES)
    step = n // nxy
    r, c = place_of()
    core, zh = lax.rem(r, CORES), lax.div(r, CORES)
    zl, here = lax.div(c, nxy), lax.rem(c, nxy)
    y, x = lax.div(here, nx), lax.rem(here, nx)
    z = zh * nzl + zl
    partner = (zh * CORES + 1 - core, c)

    def peer(d):
        oy, ox = lax.div(d, nx), lax.rem(d, nx)
        q = lax.rem(y + oy, ny) * nx + lax.rem(x + ox, nx)
        return q, (r, zl * nxy + q)

    def source_of(d):
        oy, ox = lax.div(d, nx), lax.rem(d, nx)
        return lax.rem(y + ny - oy, ny) * nx + lax.rem(x + nx - ox, nx)

    def zpeer(d):
        k = lax.rem(z + d, nz)
        return k, (lax.div(k, nzl) * CORES + core, lax.rem(k, nzl) * nxy + here)

    extra = [partner]
    extra += [peer(jnp.int32(d))[1] for d in range(1, nxy)]
    extra += [zpeer(jnp.int32(d))[1] for d in range(1, nz)]
    greet(rows, cols, extra)

    def remote(src, dst, ssem, rsem, where):
        return pltpu.make_async_remote_copy(
            src_ref=src, dst_ref=dst, send_sem=ssem, recv_sem=rsem, device_id=where, device_id_type=MESH
        )

    def band(q):
        return pl.ds(pl.multiple_of(q * step, step), step)

    def pair(d):
        q, _ = peer(d)
        return remote(
            gp_ref.at[1 - core, band(q), :], theirs.at[band(q), :], send_pair.at[d], recv_pair.at[d], partner
        )

    def spread(d):
        q, where = peer(d)
        return remote(ours.at[band(q), :], slots.at[d], send_xy.at[d], recv_xy.at[d], where)

    def each(count, body, low=0):
        def go(i, carry):
            body(count - 1 - i)
            return carry

        lax.fori_loop(0, count - low, go, 0)

    each(nxy, lambda d: pair(d).start())

    lo, hi = pl.ds(0, RIM), pl.ds(RIM + n, RIM)
    mid = pl.ds(RIM, n)
    sources = [
        gt_ref, gb_ref, gl_ref.at[mid, :], gr_ref.at[mid, :],
        gl_ref.at[lo, :], gr_ref.at[lo, :], gl_ref.at[hi, :], gr_ref.at[hi, :],
    ]
    targets = [rt, rb, rl, rr, corners.at[0], corners.at[1], corners.at[2], corners.at[3]]
    swap_rims(rows, cols, sources, targets, send_rim, recv_rim)

    def pass_on(d):
        q, _ = peer(d)
        pair(d).wait_recv()
        ours[band(q), :] = gp_ref[core, band(q), :] + theirs[band(q), :]

    def pass_and_send(d):
        pass_on(d)
        spread(d).start()

    each(nxy, pass_and_send, 1)
    pass_on(jnp.int32(0))

    finish_rims(rows, cols, sources, targets, send_rim, recv_rim)
    lane = lax.broadcasted_iota(jnp.int32, (RIM, 128), 1)
    first, final = lane < 32, lane >= 96

    def rows_of(at, up, low):
        zero = jnp.zeros((RIM, 128), jnp.float32)
        best = None
        for s in (0, 1):
            planes = []
            for q in (2 * s, 2 * s + 1):
                a = core_ref[q, pl.ds(at, RIM), 0:128]
                b = core_ref[q, pl.ds(at, RIM), 128:256]
                lft, rgt = rl[pl.ds(at, RIM), :], rr[pl.ds(at, RIM), :]
                if up is not None:
                    lft, rgt = lft + corners[up], rgt + corners[up + 1]
                if low is not None:
                    a, b = a + low[q, :, 0:128], b + low[q, :, 128:256]
                lft = pltpu.roll(lft, (128 - 32 * q) % 128, 1) if q else lft
                rgt = pltpu.roll(rgt, (96 - 32 * q) % 128, 1) if q < 3 else rgt
                a = a + jnp.where(first, lft, zero)
                b = b + jnp.where(final, rgt, zero)
                descent_ref[q, pl.ds(at, RIM), 0:128] = a
                descent_ref[q, pl.ds(at, RIM), 128:256] = b
                planes.append((a, b))
            for t in (0, 1):
                v = planes[0][t] * planes[0][t] + planes[1][t] * planes[1][t]
                best = v if best is None else jnp.maximum(best, v)
        return functools.reduce(jnp.maximum, [best[8 * k : 8 * k + 8] for k in range(RIM // 8)])

    peak = jnp.maximum(rows_of(0, 0, rt), rows_of(n - RIM, 2, rb))
    peak = lax.fori_loop(
        1, n // RIM - 1, lambda i, m: jnp.maximum(m, rows_of(pl.multiple_of(i * RIM, RIM), None, None)), peak
    )
    zpeak[pl.ds(z, 1)] = peak[None]

    def to_z(d):
        return remote(mine, zslots.at[z], send_z.at[d], recv_z.at[d], zpeer(d)[1])

    def peak_to_z(d):
        return remote(zpeak.at[z], zpeak.at[z], send_zm.at[d], recv_zm.at[d], zpeer(d)[1])

    each(nz, lambda d: peak_to_z(d).start(), 1)
    each(nxy, lambda d: spread(d).wait_recv(), 1)
    acc = ours[band(here), :]
    for d in range(1, nxy):
        acc = acc + slots[d]
    mine[...] = acc
    zslots[pl.ds(z, 1)] = acc[None]
    each(nz, lambda d: to_z(d).start(), 1)

    def z_arrived(d):
        to_z(d).wait_recv()
        peak_to_z(d).wait_recv()

    each(nz, z_arrived, 1)
    acc = zslots[0]
    peak = zpeak[0]
    for k in range(1, nz):
        acc = acc + zslots[k]
        peak = jnp.maximum(peak, zpeak[k])
    total_ref[pl.ds(core, 1), band(here), :] = acc[None]
    xpeak[0] = peak

    def to_all(d):
        block = total_ref.at[core, band(here), :]
        return remote(block, block, send_all.at[d], recv_all.at[d], peer(d)[1])

    def peak_to_all(d):
        return remote(xpeak.at[0], xpeak.at[d], send_xm.at[d], recv_xm.at[d], peer(d)[1])

    def back(d):
        q = source_of(d)
        block = total_ref.at[core, band(q), :]
        return remote(block, block, send_back.at[d], recv_back.at[d], partner)

    def start_all(d):
        to_all(d).start()
        peak_to_all(d).start()

    def arrived(d):
        q = source_of(d)
        block = total_ref.at[core, band(q), :]
        remote(block, block, send_all.at[d], recv_all.at[d], partner).wait_recv()
        back(d).start()

    each(nxy, start_all, 1)
    back(jnp.int32(0)).start()

    lax.fori_loop(1, nxy, lambda d, carry: (arrived(d), carry)[1], 0)
    each(nxy, lambda d: peak_to_all(d).wait_recv(), 1)
    peak = xpeak[0]
    for d in range(1, nxy):
        peak = jnp.maximum(peak, xpeak[d])
    ppeak[0] = peak
    last = remote(ppeak.at[0], ppeak.at[1], send_pm, recv_pm, partner)
    last.start()
    last.wait()
    peak_ref[...] = jnp.maximum(ppeak[0], ppeak[1])

    def drain(d):
        pair(d).wait_send()
        back(d).wait()

    def drain_xy(d):
        spread(d).wait_send()
        to_all(d).wait_send()
        peak_to_all(d).wait_send()

    def drain_z(d):
        to_z(d).wait_send()
        peak_to_z(d).wait_send()

    each(nxy, drain)
    each(nxy, drain_xy, 1)
    each(nz, drain_z, 1)


def local(rows, cols, nyx, table, perm, object_in, probe_in, positions, intensity):
    n = probe_in.shape[-1]
    npos = positions.shape[2]
    f32 = jnp.float32
    obj = object_in.reshape(4, n, n)
    vmem = pl.BlockSpec(memory_space=pltpu.VMEM)
    smem = pl.BlockSpec(memory_space=pltpu.SMEM)
    dma = pltpu.SemaphoreType.DMA
    rim = jax.ShapeDtypeStruct((4, RIM, n), f32)
    side = jax.ShapeDtypeStruct((n + 2 * RIM, 128), f32)
    field = jax.ShapeDtypeStruct((4, n, n), f32)
    wave = jax.ShapeDtypeStruct((2, n, n), f32)
    top, bottom, left, right = pl.pallas_call(
        functools.partial(halo_kernel, rows, cols),
        out_shape=(rim, rim, side, side),
        in_specs=[vmem],
        out_specs=(vmem,) * 4,
        scratch_shapes=[VMEM((n, 128), f32), VMEM((n, 128), f32), dma((8,)), dma((8,))],
        compiler_params=pltpu.CompilerParams(collective_id=0, has_side_effects=True),
        name="halo",
    )(obj)
    core, gt, gb, gl, gr, gp = pl.pallas_call(
        tile_kernel,
        out_shape=(field, rim, rim, side, side, wave),
        in_specs=[smem] + [vmem] * 9,
        out_specs=(vmem,) * 6,
        scratch_shapes=[
            VMEM((4, 4, n + 2 * RIM, 128), f32),
            VMEM((npos, 4, n, n), f32),
            VMEM((npos, 2, n, n), f32),
            VMEM((npos, 4, 2, n + 128, 128), f32),
            VMEM((npos, 2, n, 128), f32),
        ],
        compiler_params=pltpu.CompilerParams(vmem_limit_bytes=48 * 2**20),
        name="tile",
    )(
        positions.reshape(-1), obj, top, bottom, left, right, probe_in, intensity.reshape(npos, n, n),
        jnp.asarray(table), jnp.asarray(perm),
    )
    nxy = nyx[0] * nyx[1]
    nz = rows * cols // (CORES * nxy)
    step = n // nxy
    total, descent, peak = pl.pallas_call(
        functools.partial(sum_kernel, rows, cols, nyx),
        out_shape=(wave, field, jax.ShapeDtypeStruct((8, 128), f32)),
        in_specs=[vmem] * 6,
        out_specs=(vmem,) * 3,
        scratch_shapes=[
            VMEM((n, n), f32), VMEM((n, n), f32), VMEM((nxy, step, n), f32), VMEM((nz, step, n), f32),
            VMEM((step, n), f32), VMEM((nz, 8, 128), f32), VMEM((nxy, 8, 128), f32), VMEM((2, 8, 128), f32),
            VMEM((4, RIM, n), f32), VMEM((4, RIM, n), f32), VMEM((n, 128), f32), VMEM((n, 128), f32),
            VMEM((4, RIM, 128), f32),
            dma((8,)), dma((8,)), dma((nxy,)), dma((nxy,)), dma((nxy,)), dma((nxy,)), dma((nz,)), dma((nz,)),
            dma((nz,)), dma((nz,)), dma((nxy,)), dma((nxy,)), dma((nxy,)), dma((nxy,)), dma((nxy,)), dma((nxy,)),
            dma, dma,
        ],
        compiler_params=pltpu.CompilerParams(collective_id=1, has_side_effects=True),
        name="sums",
    )(gp, core, gt, gb, gl, gr)
    tiles = rows * cols
    largest = jnp.max(peak)
    descent = descent.reshape(object_in.shape)
    object_out = object_in - 0.3 * descent / (jnp.sqrt(largest) + 1e-06)
    probe_out = probe_in - (2.0 / tiles) * total
    return object_out, probe_out


def solution(mesh):
    rows, cols = mesh.shape["row"], mesh.shape["col"]
    table, perm = weights(256)
    spec = (P(None, None, "row", "col"), P(), P("row", "col", None, None), P("row", "col", None, None, None))
    return jax.shard_map(
        functools.partial(local, rows, cols, NYX, table, perm),
        mesh=mesh,
        in_specs=spec,
        out_specs=(P(None, None, "row", "col"), P()),
        check_vma=False,
    )
```

time: 402 us -> 90.2 us (0.22); the launches traced: 396 us -> 89.7 us
  waiting for transfers between devices: 145 us -> 0 us
  matrix products: 94.1 us -> 0 us
  Pallas kernels: 0 us -> 71.4 us
  local copies, waits for them, and re-layouts: 56.8 us -> 12.3 us
  blocking collectives: 40.6 us -> 0 us
  starting transfers between devices: 25 us -> 0 us
  between operations: 20.4 us -> 1.4 us
  other arithmetic: 13.9 us -> 4.59 us
    psum x5 -> x0, waiting for transfers between devices: 117 us -> none  [by_axis(): array = lax.psum(array, axis)]
    dot_general x48 -> x0, matrix products: 94.1 us -> none  [the longest x6 13.1 us: transform(): ic = jnp.einsum('byx,xk->byk', imag_part, cosine, precision=high)]
    pallas_call x0 -> x3, Pallas kernels: none -> 71.4 us  [the longest x1 40.4 us: local(): pl.pallas_call(functools.partial(sum_kernel, rows, cols, nyx), out_shape=...]
    pmax x5 -> x0, blocking collectives: 40.6 us -> none  [one_axis_at_a_time(): array = lax.pmax(array, axis)]
    dynamic_update_slice x2 -> x0, local copies, waits for them, and re-layouts: 27.3 us -> none  [tile_gradient(): lax.dynamic_update_slice(gradient, current + pieces[position], start_at)]
    ppermute x8 -> x0, waiting for transfers between devices: 27.2 us -> none  [the longest x2 14.2 us: extended(): lax.ppermute(head, axis, [((i + 1) % count, i) for i in range(ends)])]
    ppermute x8 -> x0, starting transfers between devices: 24.8 us -> none  [the longest x4 12.1 us: passed_along(): lax.ppermute(value, axis, [(source, source + steps) for source in range(i...]
    gather x20 -> x0, local copies, waits for them, and re-layouts: 10.8 us -> none
  transfers between devices with their start and end apart: 13 -> 0, of which waited for: 10 -> 0; matrix products, arithmetic and copies ran while one was open for 13% -> 0% of each run, Pallas kernels for 0% -> 0%
where the time goes in v1:
time: 90.2 us; the launch traced here: 89.7 us
  Pallas kernels  71.4 us (79%)
  local copies, waits for them, and re-layouts  12.3 us (14%)
  other arithmetic  4.59 us (5%)
  between operations  1.4 us (2%)
    pallas_call x1, Pallas kernels, local(): pl.pallas_call(functools.partial(sum_kernel, rows, cols, nyx), out_shape=...  40.4 us
    pallas_call x1, Pallas kernels, local(): pl.pallas_call(tile_kernel, out_shape=(field, rim, rim, side, side, wave)...  17.2 us
    pallas_call x1, Pallas kernels, local(): pl.pallas_call(functools.partial(halo_kernel, rows, cols), out_shape=(rim...  13.8 us
    unnamed x32, local copies, waits for them, and re-layouts  11.5 us

profile of v1, /device:TPU:1, one launch (start us, length us, event | category | flops | bytes accessed | tf_op | source)
XLA Modules:
  0.0 89.7 jit_solution(10813906072368652510)
XLA Ops:
  0.6 0.0 copy-start
  0.6 0.8 reshape.18.pos_ref
  1.5 13.8 %halo.1 = (f32[4,32,256]{2,1,0:T(8,128)}, f32[4,32,256]{2,1,0:T(8,128)}, f32[320,128]{1,0:T(8,128)}, f32[320,128]{1,0:T(8,128)}) custom-call(f32[4,256,256]{2,1,0:T(8,128)} %bitcast.3), custom_call_target="tpu_custom_call" | custom-call | tf_op jit(solution)/shard_map/halo/pallas_call | solution.py:568
  15.3 0.0 copy-done
  15.3 0.0 copy-start.1
  15.3 1.0 %copy-done.1 = f32[2,256,256]{2,1,0:T(8,128)S(1)} copy-done((f32[2,256,256]{2,1,0:T(8,128)S(1)}, f32[2,256,256]{2,1,0:T(8,128)}, u32[]{:S(2)}) %copy-start.1) | copy-done | bytes 524312
  16.4 0.0 copy-start.4
  16.4 1.0 %copy-done.4 = f32[1,1,2,256,256]{4,3,2,1,0:T(8,128)S(1)} copy-done((f32[1,1,2,256,256]{4,3,2,1,0:T(8,128)S(1)}, f32[1,1,2,256,256]{4,3,2,1,0:T(8,128)}, u32[]{:S(2)}) %copy-start.4) | copy-done | bytes 524312
  17.4 0.0 copy-start.8
  17.4 0.9 %copy-done.8 = f32[320,128]{1,0:T(8,128)S(1)} copy-done((f32[320,128]{1,0:T(8,128)S(1)}, f32[320,128]{1,0:T(8,128)}, u32[]{:S(2)}) %copy-start.8) | copy-done | bytes 163864
  18.3 0.0 copy-start.9
  18.3 0.9 %copy-done.9 = f32[320,128]{1,0:T(8,128)S(1)} copy-done((f32[320,128]{1,0:T(8,128)S(1)}, f32[320,128]{1,0:T(8,128)}, u32[]{:S(2)}) %copy-start.9) | copy-done | bytes 163864
  19.3 0.0 copy-start.10
  19.3 0.9 %copy-done.10 = bf16[256,256]{1,0:T(8,128)(2,1)S(1)} copy-done((bf16[256,256]{1,0:T(8,128)(2,1)S(1)}, bf16[256,256]{1,0:T(8,128)(2,1)}, u32[]{:S(2)}) %copy-start.10) | copy-done | bytes 131096
  20.2 0.0 copy-start.13
  20.2 0.9 %copy-done.13 = f32[4,32,256]{2,1,0:T(8,128)S(1)} copy-done((f32[4,32,256]{2,1,0:T(8,128)S(1)}, f32[4,32,256]{2,1,0:T(8,128)}, u32[]{:S(2)}) %copy-start.13) | copy-done | bytes 131096
  21.1 0.0 copy-start.14
  21.1 0.9 %copy-done.14 = f32[4,32,256]{2,1,0:T(8,128)S(1)} copy-done((f32[4,32,256]{2,1,0:T(8,128)S(1)}, f32[4,32,256]{2,1,0:T(8,128)}, u32[]{:S(2)}) %copy-start.14) | copy-done | bytes 131096
  22.0 17.2 %tile.1 = (f32[4,256,256]{2,1,0:T(8,128)S(1)}, f32[4,32,256]{2,1,0:T(8,128)S(1)}, f32[4,32,256]{2,1,0:T(8,128)S(1)}, f32[320,128]{1,0:T(8,128)S(1)}, f32[320,128]{1,0:T(8,128)S(1)}, /*index=5*/f32[2,256,256]{2,1,0:T(8,128)S(1)}) custom-call(s32[4]{0:T(128)S(1)} %reshape.18.pos_ref, f32[4,256,256]{2,1,0:T(8,128)S(1)} %bitcast.4, ...), custom_call_target="tpu_custom_call" | custom-call | tf_op jit(solution)/shard_map/tile/pallas_call | solution.py:577
  39.2 0.0 copy-start.3
  39.2 1.0 %copy-done.3 = f32[4,256,256]{2,1,0:T(8,128)} copy-done((f32[4,256,256]{2,1,0:T(8,128)}, f32[4,256,256]{2,1,0:T(8,128)S(1)}, u32[]{:S(2)}) %copy-start.3) | copy-done | bytes 1048600
  40.2 0.0 copy-start.5
  40.2 0.8 copy-done.5
  41.0 0.0 copy-start.6
  41.0 0.7 copy-done.6
  41.6 0.0 copy-start.7
  41.6 0.7 copy-done.7
  42.3 0.0 copy-start.11
  42.3 0.7 copy-done.11
  42.9 0.0 copy-start.12
  42.9 0.6 copy-done.12
  43.6 40.4 %sums.1 = (f32[2,256,256]{2,1,0:T(8,128)}, f32[4,256,256]{2,1,0:T(8,128)}, f32[8,128]{1,0:T(8,128)}) custom-call(f32[2,256,256]{2,1,0:T(8,128)} %copy-done.5, f32[4,256,256]{2,1,0:T(8,128)} %copy-done.3, f32[4,32,256]{2,1,0:T(8,128)} %copy-done.11, f32[4,32,256]{2,1,0:T(8,128)} %copy-done.12, f32[320,128]{1,0:T(8,128)} %copy-done.6, f32[320,128]{1,0:T(8,128)} %copy-done.7), custom_call_target="tpu_custom_call" | custom-call | tf_op jit(solution)/shard_map/sums/pallas_call | solution.py:598
  84.0 1.3 %reduce_max.9 = f32[]{:T(128)} reduce(f32[8,128]{1,0:T(8,128)} %get-tuple-element.26, f32[]{:T(128)} %constant.3.clone.1), dimensions={0,1}, to_apply=%region_0.0 | reduce | flops 1023 | bytes 4104 | tf_op jit(solution)/shard_map/reduce_max | solution.py:616
  86.0 1.3 %multiply_divide_fusion = f32[4,256,256]{2,1,0:T(8,128)S(1)} fusion(f32[4,256,256]{2,1,0:T(8,128)} %get-tuple-element.25, f32[]{:T(128)S(6)} %add.3), kind=kLoop, calls=%fused_computation | loop fusion | flops 524288 | bytes 2097156 | tf_op jit(solution)/shard_map/div | solution.py:618
  87.3 0.0 copy-start.2
  87.3 0.0 copy-start.15
  87.3 1.1 %sub.6 = f32[2,2,256,256]{3,2,1,0:T(8,128)} subtract(f32[2,2,256,256]{3,2,1,0:T(8,128)S(1)} %copy-done, f32[2,2,256,256]{3,2,1,0:T(8,128)S(1)} %bitcast.6) | non-fusion elementwise | flops 262144 | bytes 3145728 | tf_op jit(solution)/shard_map/sub | solution.py:618
  88.4 0.0 copy-done.2
  88.4 0.4 copy-done.15
  88.9 0.9 multiply_subtract_fusion
Async XLA Ops:
  0.6 14.7 %copy-start = (f32[2,2,256,256]{3,2,1,0:T(8,128)S(1)}, f32[2,2,256,256]{3,2,1,0:T(8,128)}, u32[]{:S(2)}) copy-start(f32[2,2,256,256]{3,2,1,0:T(8,128)} %param.6) | copy-start | bytes 3145732
  15.3 1.0 %copy-start.1 = (f32[2,256,256]{2,1,0:T(8,128)S(1)}, f32[2,256,256]{2,1,0:T(8,128)}, u32[]{:S(2)}) copy-start(f32[2,256,256]{2,1,0:T(8,128)} %probe_ref.1) | copy-start | bytes 1572868
  16.4 1.0 %copy-start.4 = (f32[1,1,2,256,256]{4,3,2,1,0:T(8,128)S(1)}, f32[1,1,2,256,256]{4,3,2,1,0:T(8,128)}, u32[]{:S(2)}) copy-start(f32[1,1,2,256,256]{4,3,2,1,0:T(8,128)} %param.9) | copy-start | bytes 1572868
  17.4 0.9 %copy-start.8 = (f32[320,128]{1,0:T(8,128)S(1)}, f32[320,128]{1,0:T(8,128)}, u32[]{:S(2)}) copy-start(f32[320,128]{1,0:T(8,128)} %get-tuple-element.17.left_ref) | copy-start | bytes 491524
  18.3 0.9 %copy-start.9 = (f32[320,128]{1,0:T(8,128)S(1)}, f32[320,128]{1,0:T(8,128)}, u32[]{:S(2)}) copy-start(f32[320,128]{1,0:T(8,128)} %get-tuple-element.18.right_ref) | copy-start | bytes 491524
  19.3 0.9 %copy-start.10 = (bf16[256,256]{1,0:T(8,128)(2,1)S(1)}, bf16[256,256]{1,0:T(8,128)(2,1)}, u32[]{:S(2)}) copy-start(bf16[256,256]{1,0:T(8,128)(2,1)} %constant.13.clone.perm_ref) | copy-start | bytes 393220
  20.2 0.9 %copy-start.13 = (f32[4,32,256]{2,1,0:T(8,128)S(1)}, f32[4,32,256]{2,1,0:T(8,128)}, u32[]{:S(2)}) copy-start(f32[4,32,256]{2,1,0:T(8,128)} %get-tuple-element.15.top_ref) | copy-start | bytes 393220
  21.1 0.9 %copy-start.14 = (f32[4,32,256]{2,1,0:T(8,128)S(1)}, f32[4,32,256]{2,1,0:T(8,128)}, u32[]{:S(2)}) copy-start(f32[4,32,256]{2,1,0:T(8,128)} %get-tuple-element.16.bottom_ref) | copy-start | bytes 393220
  39.2 1.0 %copy-start.3 = (f32[4,256,256]{2,1,0:T(8,128)}, f32[4,256,256]{2,1,0:T(8,128)S(1)}, u32[]{:S(2)}) copy-start(f32[4,256,256]{2,1,0:T(8,128)S(1)} %get-tuple-element.20.core_ref) | copy-start | bytes 3145732
  40.2 0.8 copy-start.5
  41.0 0.7 copy-start.6
  41.6 0.7 copy-start.7
  42.3 0.7 copy-start.11
  42.9 0.6 copy-start.12
  87.3 1.1 %copy-start.2 = (f32[2,256,256]{2,1,0:T(8,128)S(1)}, f32[2,256,256]{2,1,0:T(8,128)}, u32[]{:S(2)}) copy-start(f32[2,256,256]{2,1,0:T(8,128)} %probe_ref.1) | copy-start | bytes 1572868
  87.3 1.5 %copy-start.15 = (f32[2,256,256]{2,1,0:T(8,128)S(1)}, f32[2,256,256]{2,1,0:T(8,128)}, u32[]{:S(2)}) copy-start(f32[2,256,256]{2,1,0:T(8,128)} %get-tuple-element.27) | copy-start | bytes 1572868

commit v2 on v0

v2 whole, which is shorter than its diff:
```python
import functools
import math

import jax
import jax.numpy as jnp
import numpy as np
from jax import lax
from jax.experimental import pallas as pl
from jax.experimental.pallas import tpu as pltpu
from jax.sharding import PartitionSpec as P

RIM = 32
MESH = pl.DeviceIdType.MESH
VMEM = pltpu.VMEM
AROUND = ((-1, 0), (1, 0), (0, -1), (0, 1), (-1, -1), (-1, 1), (1, -1), (1, 1))
CORES = 2
NYX = (4, 4)
SUBS = 2


def split_of(matrix):
    high = matrix.astype(jnp.bfloat16)
    low = (matrix - high.astype(np.float64)).astype(jnp.bfloat16)
    return np.stack([np.asarray(high), np.asarray(low)])


def stacked(weight):
    real, imag = weight.real, weight.imag
    return np.block([[real, imag], [-imag, real]])


def weights(extent):
    half = extent // 2
    idx = np.arange(extent)
    freq = ((idx + half) % extent - half).astype(np.float64)
    turn = np.exp(-2j * np.pi * ((idx[:, None] * idx[None, :]) % extent) / extent)
    phase = np.exp(-8j * np.pi * freq**2 / extent**2)
    band = (np.conj(turn) * phase[None, :]) @ turn / extent
    left, right = band[:half, :half], band[:half, half:]
    even = turn[:half, 0::2] / math.sqrt(extent)
    odd = turn[:half, 1::2] / math.sqrt(extent)
    plus, minus = stacked((left + right) / 2), stacked((left - right) / 2)
    ev, od = stacked(even), stacked(odd)
    table = np.stack([split_of(m) for m in (plus, minus, ev, od, od.T)])
    order = np.concatenate([idx[0::2], idx[1::2]])
    perm = np.zeros((extent, extent), np.float32)
    perm[order, idx] = 1.0
    return table, perm.astype(jnp.bfloat16)


def parts(x):
    high = x.astype(jnp.bfloat16)
    return high, (x - high.astype(jnp.float32)).astype(jnp.bfloat16)


def dot(a, b):
    return jnp.dot(a, b, preferred_element_type=jnp.float32)


def times_right(x, w_ref, k):
    high, low = parts(x)
    wh, wl = w_ref[k, 0], w_ref[k, 1]
    return dot(jnp.concatenate([high, low, high], 1), jnp.concatenate([wh, wh, wl], 0))


def times_left(x, w_ref, k):
    high, low = parts(x)
    wh, wl = w_ref[k, 0], w_ref[k, 1]
    return dot(jnp.concatenate([wh, wh, wl], 1), jnp.concatenate([high, low, high], 0))


def fold(x):
    h = x.shape[0] // 2
    s, d = x[:h] + x[h:], x[:h] - x[h:]
    return [[s[:, :h] + s[:, h:], s[:, :h] - s[:, h:]], [d[:, :h] + d[:, h:], d[:, :h] - d[:, h:]]]


def unfold(b):
    top_s, top_d = b[0][0] + b[0][1], b[0][0] - b[0][1]
    bot_s, bot_d = b[1][0] + b[1][1], b[1][0] - b[1][1]
    s = jnp.concatenate([top_s, top_d], 1)
    d = jnp.concatenate([bot_s, bot_d], 1)
    return jnp.concatenate([s + d, s - d], 0)


def sandwich(re, im, w_ref, right, left):
    h = re[0][0].shape[0]
    out = [None, None]
    for j in (0, 1):
        k, swap = right[j]
        first, second = (im, re) if swap else (re, im)
        x = jnp.concatenate(
            [jnp.concatenate([first[i][j], second[i][j]], 1) for i in (0, 1)], 0
        )
        y = times_right(x, w_ref, k)
        a, b = y[:, :h], y[:, h:]
        out[j] = (b, a) if swap else (a, b)
    res_re, res_im = [None, None], [None, None]
    for i in (0, 1):
        k, swap = left[i]
        rows = slice(i * h, (i + 1) * h)
        r = jnp.concatenate([out[0][0][rows], out[1][0][rows]], 1)
        m = jnp.concatenate([out[0][1][rows], out[1][1][rows]], 1)
        y = times_left(jnp.concatenate([m, r] if swap else [r, m], 0), w_ref, k)
        a, b = y[:h], y[h:]
        r, m = (b, a) if swap else (a, b)
        res_re[i] = [r[:, :h], r[:, h:]]
        res_im[i] = [m[:, :h], m[:, h:]]
    return res_re, res_im


PROP = (((0, False), (1, False)), ((0, True), (1, True)))
PROP_CONJ = (((0, True), (1, True)), ((0, False), (1, False)))
FORWARD = (((2, False), (3, False)), ((2, True), (4, False)))
BACKWARD = (((2, True), (4, False)), ((2, False), (3, False)))


def rows_at(start, size):
    return pl.ds(pl.multiple_of(start, size), size)


def place_of():
    return lax.axis_index("row"), lax.axis_index("col")


def neighbours(rows, cols):
    r, c = place_of()
    out = []
    for dr, dc in AROUND:
        ok = None
        if dr:
            ok = r > 0 if dr < 0 else r < rows - 1
        if dc:
            side = c > 0 if dc < 0 else c < cols - 1
            ok = side if ok is None else jnp.logical_and(ok, side)
        out.append((ok, (r + dr, c + dc)))
    return out


def opposite(d):
    dr, dc = AROUND[d]
    return AROUND.index((-dr, -dc))


def remote(src, dst, ssem, rsem, where):
    return pltpu.make_async_remote_copy(
        src_ref=src, dst_ref=dst, send_sem=ssem, recv_sem=rsem, device_id=where, device_id_type=MESH
    )


def greet(around, extra):
    barrier = pltpu.get_barrier_semaphore()
    for ok, where in around:

        @pl.when(ok)
        def _(where=where):
            pl.semaphore_signal(barrier, inc=1, device_id=where, device_id_type=MESH)

    for where in extra:
        pl.semaphore_signal(barrier, inc=1, device_id=where, device_id_type=MESH)


def await_greetings(rows, cols, extra):
    r, c = place_of()
    tall = 1 + jnp.where(r > 0, 1, 0) + jnp.where(r < rows - 1, 1, 0)
    wide = 1 + jnp.where(c > 0, 1, 0) + jnp.where(c < cols - 1, 1, 0)
    pl.semaphore_wait(pltpu.get_barrier_semaphore(), tall * wide - 1 + len(extra))


def swap_rims(around, sources, targets, send_sem, recv_sem):
    for d, (ok, where) in enumerate(around):
        o = opposite(d)
        copy = remote(sources[d], targets[o], send_sem.at[d], recv_sem.at[o], where)
        pl.when(ok)(copy.start)
        target = targets[d]

        @pl.when(jnp.logical_not(ok))
        def _(target=target):
            target[...] = jnp.zeros(target.shape, target.dtype)


def finish_rims(around, sources, targets, send_sem, recv_sem):
    for d, (ok, where) in enumerate(around):
        pl.when(ok)(remote(sources[d], targets[d], send_sem.at[d], recv_sem.at[d], where).wait)


def both(ref, *at):
    return jnp.concatenate([ref[(*at, 0)], ref[(*at, 1)]], 1)


def pack_sides(first, last, quarter):
    left, right = first(0), pltpu.roll(last(0), 32, 1)
    for q in range(1, 4):
        left = jnp.where(quarter == q, pltpu.roll(first(q), 32 * q, 1), left)
        right = jnp.where(quarter == q, pltpu.roll(last(q), (32 * q + 32) % 128, 1), right)
    return left, right


def kernel(
    rows, cols, nyx,
    pos_ref, obj_ref, probe_in, meas_in, table_in, perm_in,
    obj_out, probe_out,
    probe_ref, meas_ref, w_ref, perm_ref,
    win, pl_buf, pr_buf, hl, hr,
    cut, mid, pad, seen,
    grad, gl, gr, gp_ref, fresh,
    theirs, ours, slots, mine, zslots, zpeak, xpeak, ppeak, total_ref,
    rt, rb, rl, rr, corners,
    load_sem, store_sem,
    send_halo, recv_halo, send_rim, recv_rim, send_pair, recv_pair, send_xy, recv_xy, send_z, recv_z,
    send_zm, recv_zm, send_xm, recv_xm, send_all, recv_all, send_back, recv_back, send_pm, recv_pm,
):
    n = probe_ref.shape[-1]
    h = n // 2
    npos = cut.shape[0]
    ny, nx = nyx
    nxy = ny * nx
    nzl = cols // nxy
    nz = nzl * (rows // CORES)
    step = n // nxy // SUBS
    r, c = place_of()
    core, zh = lax.rem(r, CORES), lax.div(r, CORES)
    zl, here = lax.div(c, nxy), lax.rem(c, nxy)
    y, x = lax.div(here, nx), lax.rem(here, nx)
    z = zh * nzl + zl
    partner = (zh * CORES + 1 - core, c)

    def peer(d):
        oy, ox = lax.div(d, nx), lax.rem(d, nx)
        q = lax.rem(y + oy, ny) * nx + lax.rem(x + ox, nx)
        return q, (r, zl * nxy + q)

    def source_of(d):
        oy, ox = lax.div(d, nx), lax.rem(d, nx)
        return lax.rem(y + ny - oy, ny) * nx + lax.rem(x + nx - ox, nx)

    def zpeer(d):
        k = lax.rem(z + d, nz)
        return lax.div(k, nzl) * CORES + core, lax.rem(k, nzl) * nxy + here

    def each(count, body, low=0):
        def go(i, carry):
            body(count - 1 - i)
            return carry

        lax.fori_loop(0, count - low, go, 0)

    around = neighbours(rows, cols)
    extra = [partner]
    extra += [peer(jnp.int32(d))[1] for d in range(1, nxy)]
    extra += [zpeer(jnp.int32(d)) for d in range(1, nz)]
    greet(around, extra)

    inner = pl.ds(RIM, n)
    loads = [
        (obj_ref.at[:, :, pl.ds(0, 128)], win.at[:, 1, inner, :]),
        (obj_ref.at[:, :, pl.ds(128, 128)], win.at[:, 2, inner, :]),
        (meas_in, meas_ref),
        (perm_in, perm_ref),
        (probe_in, probe_ref),
        (table_in, w_ref),
    ]
    loads = [pltpu.make_async_copy(a, b, load_sem.at[i]) for i, (a, b) in enumerate(loads)]
    for load in loads:
        load.start()
    loads[0].wait()
    loads[1].wait()
    quarter = lax.div(lax.broadcasted_iota(jnp.int32, (n, 128), 1), 32)
    pl_buf[...], pr_buf[...] = pack_sides(
        lambda q: win[q, 1, RIM : RIM + n, :], lambda q: win[q, 2, RIM : RIM + n, :], quarter
    )
    await_greetings(rows, cols, extra)

    ups, tops = pl.ds(0, RIM), pl.ds(RIM, RIM)
    lows, downs = pl.ds(n, RIM), pl.ds(n + RIM, RIM)
    lo, hi = pl.ds(0, RIM), pl.ds(n - RIM, RIM)
    halo = (
        around,
        [
            win.at[:, 1:3, tops, :], win.at[:, 1:3, lows, :], pl_buf, pr_buf,
            pl_buf.at[lo, :], pr_buf.at[lo, :], pl_buf.at[hi, :], pr_buf.at[hi, :],
        ],
        [
            win.at[:, 1:3, ups, :], win.at[:, 1:3, downs, :], hl.at[inner, :], hr.at[inner, :],
            hl.at[ups, :], hr.at[ups, :], hl.at[downs, :], hr.at[downs, :],
        ],
        send_halo,
        recv_halo,
    )
    swap_rims(*halo)

    zeros = jnp.zeros((64, 128), jnp.float32)
    for p in range(npos):
        for q in range(4):
            for t in (0, 1):
                pad[p, q, t, 0:64, :] = zeros
                pad[p, q, t, 64 + n :, :] = zeros
    loads[2].wait()
    loads[3].wait()
    for p in range(npos):
        for t in (0, 1):
            seen[p, t] = meas_ref[p, :, 128 * t : 128 * t + 128]
        meas = jnp.concatenate(
            [
                jnp.concatenate([seen[p, t, pl.ds(i, h, stride=2), :] for t in (0, 1)], 1)
                for i in (0, 1)
            ],
            0,
        )
        mh, ml = parts(meas)
        meas_ref[p] = dot(
            jnp.concatenate([mh, ml], 1), jnp.concatenate([perm_ref[...], perm_ref[...]], 0)
        )
    loads[4].wait()
    loads[5].wait()
    finish_rims(*halo)
    for q in range(4):
        win[q, 0] = pltpu.roll(hl[...], (96 - 32 * q) % 128, 1)
        win[q, 3] = pltpu.roll(hr[...], (128 - 32 * q) % 128, 1) if q else hr[...]

    offs = [(pos_ref[2 * p], pos_ref[2 * p + 1]) for p in range(npos)]
    lane = lax.broadcasted_iota(jnp.int32, (RIM, 128), 1)

    def cut_rows(i, carry):
        for p in range(npos):
            dy, dx = offs[p]
            shift = lax.rem(128 - dx, 128)
            high, low = lane >= 128 - dx, lane < -dx
            for q in range(4):
                at = pl.ds(RIM + dy + i * RIM, RIM)
                t0, t1, t2, t3 = [pltpu.roll(win[q, t, at, :], shift, 1) for t in range(4)]
                to = rows_at(i * RIM, RIM)
                cut[p, q, 0, to, :] = jnp.where(high, t2, jnp.where(low, t0, t1))
                cut[p, q, 1, to, :] = jnp.where(high, t3, jnp.where(low, t1, t2))
        return carry

    lax.fori_loop(0, n // RIM, cut_rows, 0)

    def keep(p, q, value):
        pad[p, q, 0, 64 : 64 + n, :] = value[:, :128]
        pad[p, q, 1, 64 : 64 + n, :] = value[:, 128:]

    for p in range(npos):
        pr, pi = probe_ref[0], probe_ref[1]
        ar, ai = both(cut, p, 0), both(cut, p, 1)
        re, im = sandwich(fold(pr * ar - pi * ai), fold(pr * ai + pi * ar), w_ref, *PROP)
        qr, qi = unfold(re), unfold(im)
        mid[p, 0], mid[p, 1] = qr, qi
        br, bi = both(cut, p, 2), both(cut, p, 3)
        re, im = sandwich(fold(qr * br - qi * bi), fold(qr * bi + qi * br), w_ref, *FORWARD)
        for i in (0, 1):
            for j in (0, 1):
                fr, fi = re[i][j], im[i][j]
                seen_at = meas_ref[p, i * h : (i + 1) * h, j * h : (j + 1) * h]
                ex = 2.0 * (fr * fr + fi * fi - seen_at)
                re[i][j], im[i][j] = ex * fr, ex * fi
        re, im = sandwich(re, im, w_ref, *BACKWARD)
        hr_, hi_ = unfold(re), unfold(im)
        qr, qi = mid[p, 0], mid[p, 1]
        keep(p, 2, qr * hr_ + qi * hi_)
        keep(p, 3, qr * hi_ - qi * hr_)
        br, bi = both(cut, p, 2), both(cut, p, 3)
        re, im = sandwich(fold(br * hr_ + bi * hi_), fold(br * hi_ - bi * hr_), w_ref, *PROP_CONJ)
        er, ei = unfold(re), unfold(im)
        pr, pi = probe_ref[0], probe_ref[1]
        keep(p, 0, pr * er + pi * ei)
        keep(p, 1, pr * ei - pi * er)
        ar, ai = both(cut, p, 0), both(cut, p, 1)
        if p == 0:
            gp_ref[0] = ar * er + ai * ei
            gp_ref[1] = ar * ei - ai * er
        else:
            gp_ref[0] += ar * er + ai * ei
            gp_ref[1] += ar * ei - ai * er

    def band(q, s):
        return rows_at((q * SUBS + s) * step, step)

    def pair(s, d):
        at = band(peer(d)[0], s)
        return remote(
            gp_ref.at[1 - core, at, :], theirs.at[at, :], send_pair.at[s, d], recv_pair.at[s, d], partner
        )

    def spread(s, d):
        q, where = peer(d)
        return remote(
            ours.at[band(q, s), :], slots.at[s, d], send_xy.at[s, d], recv_xy.at[s, d], where
        )

    for s in range(SUBS):
        each(nxy, lambda d, s=s: pair(s, d).start())

    quarter = lax.div(lane, 32)

    def place(i):
        to = rows_at(i * RIM, RIM)
        ends = []
        for q in range(4):
            sums = None
            for p in range(npos):
                dy, dx = offs[p]
                shift = lax.rem(128 + dx, 128)
                low, high = lane < dx, lane >= 128 + dx
                at = pl.ds(RIM - dy + i * RIM, RIM)
                a, b = (pltpu.roll(pad[p, q, t, at, :], shift, 1) for t in (0, 1))
                o = jnp.zeros_like(a)
                got = [
                    jnp.where(high, a, o),
                    jnp.where(low, o, jnp.where(high, b, a)),
                    jnp.where(low, a, jnp.where(high, o, b)),
                    jnp.where(low, b, o),
                ]
                sums = got if sums is None else [u + v for u, v in zip(sums, got)]
            grad[q, 0, to, :] = sums[1]
            grad[q, 1, to, :] = sums[2]
            ends.append((sums[0], sums[3]))
        gr[to, :], gl[to, :] = pack_sides(lambda q: ends[q][1], lambda q: ends[q][0], quarter)

    def pass_on(s, d):
        at = band(peer(d)[0], s)
        pair(s, d).wait_recv()
        ours[at, :] = gp_ref[core, at, :] + theirs[at, :]

    def pass_and_send(s, d):
        pass_on(s, d)
        spread(s, d).start()

    for s in range(SUBS):
        each(nxy, lambda d, s=s: pass_and_send(s, d), 1)
        pass_on(s, jnp.int32(0))

    each(n // RIM + 2, place)
    rims = (
        around,
        [
            grad.at[:, :, ups, :], grad.at[:, :, downs, :], gl.at[inner, :], gr.at[inner, :],
            gl.at[ups, :], gr.at[ups, :], gl.at[downs, :], gr.at[downs, :],
        ],
        [rt, rb, rl, rr, corners.at[0], corners.at[1], corners.at[2], corners.at[3]],
        send_rim,
        recv_rim,
    )
    swap_rims(*rims)

    def to_z(s, d):
        return remote(mine.at[s], zslots.at[s, z], send_z.at[s, d], recv_z.at[s, d], zpeer(d))

    def peak_to_z(d):
        return remote(zpeak.at[z], zpeak.at[z], send_zm.at[d], recv_zm.at[d], zpeer(d))

    for s in range(SUBS):
        each(nxy, lambda d, s=s: spread(s, d).wait_recv(), 1)
        acc = ours[band(here, s), :]
        for d in range(1, nxy):
            acc = acc + slots[s, d]
        mine[s] = acc
        zslots[s, pl.ds(z, 1)] = acc[None]
        each(nz, lambda d, s=s: to_z(s, d).start(), 1)

    finish_rims(*rims)
    first, final = lane < 32, lane >= 96

    def rows_of(i, up, low):
        at, to = rows_at(i * RIM, RIM), rows_at(i * RIM + RIM, RIM)
        zero = jnp.zeros((RIM, 128), jnp.float32)
        lft, rgt = rl[at, :], rr[at, :]
        if up is not None:
            lft, rgt = lft + corners[up], rgt + corners[up + 1]
        best = None
        for l in (0, 1):
            square = [None, None]
            for q in (2 * l, 2 * l + 1):
                ends = (
                    jnp.where(first, pltpu.roll(lft, (128 - 32 * q) % 128, 1) if q else lft, zero),
                    jnp.where(final, pltpu.roll(rgt, 96 - 32 * q, 1) if q < 3 else rgt, zero),
                )
                for t in (0, 1):
                    v = grad[q, t, to, :] + ends[t]
                    if low is not None:
                        v = v + low[q, t]
                    grad[q, t, to, :] = v
                    square[t] = v * v if square[t] is None else square[t] + v * v
            for v in square:
                best = v if best is None else jnp.maximum(best, v)
        return functools.reduce(jnp.maximum, [best[8 * k : 8 * k + 8] for k in range(RIM // 8)])

    blocks = n // RIM
    peak = jnp.maximum(rows_of(0, 0, rt), rows_of(blocks - 1, 2, rb))
    peak = lax.fori_loop(1, blocks - 1, lambda i, m: jnp.maximum(m, rows_of(i, None, None)), peak)
    zpeak[pl.ds(z, 1)] = peak[None]
    each(nz, lambda d: peak_to_z(d).start(), 1)

    def to_all(s, d):
        block = total_ref.at[core, band(here, s), :]
        return remote(block, block, send_all.at[s, d], recv_all.at[s, d], peer(d)[1])

    def peak_to_all(d):
        return remote(xpeak.at[0], xpeak.at[d], send_xm.at[d], recv_xm.at[d], peer(d)[1])

    def back(s, d):
        block = total_ref.at[core, band(source_of(d), s), :]
        return remote(block, block, send_back.at[s, d], recv_back.at[s, d], partner)

    for s in range(SUBS):
        each(nz, lambda d, s=s: to_z(s, d).wait_recv(), 1)
        acc = zslots[s, 0]
        for k in range(1, nz):
            acc = acc + zslots[s, k]
        total_ref[pl.ds(core, 1), band(here, s), :] = acc[None]
        each(nxy, lambda d, s=s: to_all(s, d).start(), 1)
        back(s, jnp.int32(0)).start()

    each(nz, lambda d: peak_to_z(d).wait_recv(), 1)
    peak = zpeak[0]
    for k in range(1, nz):
        peak = jnp.maximum(peak, zpeak[k])
    xpeak[0] = peak
    each(nxy, lambda d: peak_to_all(d).start(), 1)

    def arrived(s, d):
        block = total_ref.at[core, band(source_of(d), s), :]
        remote(block, block, send_all.at[s, d], recv_all.at[s, d], partner).wait_recv()
        back(s, d).start()

    def forward(s):
        lax.fori_loop(1, nxy, lambda d, carry: (arrived(s, d), carry)[1], 0)

    for s in range(SUBS - 1):
        forward(s)
    each(nxy, lambda d: peak_to_all(d).wait_recv(), 1)
    peak = xpeak[0]
    for d in range(1, nxy):
        peak = jnp.maximum(peak, xpeak[d])
    ppeak[0] = peak
    last = remote(ppeak.at[0], ppeak.at[1], send_pm, recv_pm, partner)
    last.start()
    forward(SUBS - 1)
    last.wait()

    largest = jnp.max(jnp.maximum(ppeak[0], ppeak[1]), axis=(0, 1), keepdims=True)
    scale = jnp.broadcast_to(0.3 / (jnp.sqrt(largest) + 1e-06), (RIM, 128))

    def next_rows(i, carry):
        at = rows_at(i * RIM + RIM, RIM)
        for q in range(4):
            for t in (0, 1):
                grad[q, t, at, :] = win[q, t + 1, at, :] - scale * grad[q, t, at, :]
        return carry

    lax.fori_loop(0, blocks, next_rows, 0)
    stores = [
        pltpu.make_async_copy(grad.at[:, t, inner, :], obj_out.at[:, :, pl.ds(128 * t, 128)], store_sem.at[t])
        for t in (0, 1)
    ]
    for store in stores:
        store.start()

    def drain(s, d):
        pair(s, d).wait_send()
        back(s, d).wait()

    def drain_xy(s, d):
        spread(s, d).wait_send()
        to_all(s, d).wait_send()

    for s in range(SUBS):
        each(nxy, lambda d, s=s: drain(s, d))
    fresh[...] = probe_ref[...] - (2.0 / (rows * cols)) * total_ref[...]
    stores.append(pltpu.make_async_copy(fresh, probe_out, store_sem.at[2]))
    stores[2].start()
    for s in range(SUBS):
        each(nxy, lambda d, s=s: drain_xy(s, d), 1)
        each(nz, lambda d, s=s: to_z(s, d).wait_send(), 1)
    each(nxy, lambda d: peak_to_all(d).wait_send(), 1)
    each(nz, lambda d: peak_to_z(d).wait_send(), 1)
    for store in stores:
        store.wait()


def local(rows, cols, nyx, table, perm, object_in, probe_in, positions, intensity):
    n = probe_in.shape[-1]
    npos = positions.shape[2]
    f32 = jnp.float32
    hbm = pl.BlockSpec(memory_space=pltpu.HBM)
    smem = pl.BlockSpec(memory_space=pltpu.SMEM)
    dma = pltpu.SemaphoreType.DMA
    nxy = nyx[0] * nyx[1]
    nz = rows * cols // (CORES * nxy)
    step = n // nxy // SUBS
    wide = n + 2 * RIM
    buffers = [
        (2, n, n), (npos, n, n), table.shape, perm.shape,
        (4, 4, wide, 128), (n, 128), (n, 128), (wide, 128), (wide, 128),
        (npos, 4, 2, n, 128), (npos, 2, n, n), (npos, 4, 2, n + 128, 128), (npos, 2, n, 128),
        (4, 2, wide, 128), (wide, 128), (wide, 128), (2, n, n), (2, n, n),
        (n, n), (n, n), (SUBS, nxy, step, n), (SUBS, step, n), (SUBS, nz, step, n),
        (nz, 8, 128), (nxy, 8, 128), (2, 8, 128), (2, n, n),
        (4, 2, RIM, 128), (4, 2, RIM, 128), (n, 128), (n, 128), (4, RIM, 128),
    ]
    scratch = [VMEM(shape, jnp.bfloat16 if i in (2, 3) else f32) for i, shape in enumerate(buffers)]
    scratch += [dma((6,)), dma((3,)), dma((8,)), dma((8,)), dma((8,)), dma((8,))]
    scratch += [dma((SUBS, nxy))] * 4 + [dma((SUBS, nz))] * 2 + [dma((nz,))] * 2 + [dma((nxy,))] * 2
    scratch += [dma((SUBS, nxy))] * 4 + [dma, dma]
    object_out, probe_out = pl.pallas_call(
        functools.partial(kernel, rows, cols, nyx),
        out_shape=(jax.ShapeDtypeStruct((4, n, n), f32), jax.ShapeDtypeStruct((2, n, n), f32)),
        in_specs=[smem] + [hbm] * 5,
        out_specs=(hbm, hbm),
        scratch_shapes=scratch,
        compiler_params=pltpu.CompilerParams(
            collective_id=0, has_side_effects=True, vmem_limit_bytes=48 * 2**20
        ),
        name="step",
    )(
        positions.reshape(-1), object_in.reshape(4, n, n), probe_in, intensity.reshape(npos, n, n),
        jnp.asarray(table), jnp.asarray(perm),
    )
    return object_out.reshape(object_in.shape), probe_out


def solution(mesh):
    rows, cols = mesh.shape["row"], mesh.shape["col"]
    table, perm = weights(256)
    spec = (P(None, None, "row", "col"), P(), P("row", "col", None, None), P("row", "col", None, None, None))
    return jax.shard_map(
        functools.partial(local, rows, cols, NYX, table, perm),
        mesh=mesh,
        in_specs=spec,
        out_specs=(P(None, None, "row", "col"), P()),
        check_vma=False,
    )
```

time: 402 us -> 70.9 us (0.18); the launches traced: 396 us -> 70.6 us
  waiting for transfers between devices: 145 us -> 0 us
  matrix products: 94.1 us -> 0 us
  Pallas kernels: 0 us -> 61.9 us
  local copies, waits for them, and re-layouts: 56.8 us -> 8.05 us
  blocking collectives: 40.6 us -> 0 us
  starting transfers between devices: 25 us -> 0 us
  between operations: 20.4 us -> 0.64 us
  other arithmetic: 13.9 us -> 0 us
    psum x5 -> x0, waiting for transfers between devices: 117 us -> none  [by_axis(): array = lax.psum(array, axis)]
    dot_general x48 -> x0, matrix products: 94.1 us -> none  [the longest x6 13.1 us: transform(): ic = jnp.einsum('byx,xk->byk', imag_part, cosine, precision=high)]
    pallas_call x0 -> x1, Pallas kernels: none -> 61.9 us  [local(): pl.pallas_call(functools.partial(kernel, rows, cols, nyx), out_shape=(jax...]
    pmax x5 -> x0, blocking collectives: 40.6 us -> none  [one_axis_at_a_time(): array = lax.pmax(array, axis)]
    dynamic_update_slice x2 -> x0, local copies, waits for them, and re-layouts: 27.3 us -> none  [tile_gradient(): lax.dynamic_update_slice(gradient, current + pieces[position], start_at)]
    ppermute x8 -> x0, waiting for transfers between devices: 27.2 us -> none  [the longest x2 14.2 us: extended(): lax.ppermute(head, axis, [((i + 1) % count, i) for i in range(ends)])]
    ppermute x8 -> x0, starting transfers between devices: 24.8 us -> none  [the longest x4 12.1 us: passed_along(): lax.ppermute(value, axis, [(source, source + steps) for source in range(i...]
    gather x20 -> x0, local copies, waits for them, and re-layouts: 10.8 us -> none
  transfers between devices with their start and end apart: 13 -> 0, of which waited for: 10 -> 0; matrix products, arithmetic and copies ran while one was open for 13% -> 0% of each run, Pallas kernels for 0% -> 0%
where the time goes in v2:
time: 70.9 us; the launch traced here: 70.6 us
  Pallas kernels  61.9 us (87%)
  local copies, waits for them, and re-layouts  8.05 us (11%)
    pallas_call x1, Pallas kernels, local(): pl.pallas_call(functools.partial(kernel, rows, cols, nyx), out_shape=(jax...  61.9 us
    unnamed x12, local copies, waits for them, and re-layouts  7.29 us

profile of v2, /device:TPU:1, one launch (start us, length us, event | category | flops | bytes accessed | tf_op | source)
XLA Modules:
  0.0 70.6 jit_solution(3538992659202359593)
XLA Ops:
  0.6 0.8 %reshape.16.pos_ref = s32[4]{0:T(128)S(1)} reshape(s32[1,1,2,2]{3,2,1,0:T(2,128)} %param.8) | data formatting | bytes 32 | tf_op jit(solution)/shard_map/reshape | solution.py:616
  1.4 0.0 copy-start
  1.4 1.3 %copy-done = bf16[5,2,256,256]{3,2,1,0:T(8,128)(2,1)S(1)} copy-done((bf16[5,2,256,256]{3,2,1,0:T(8,128)(2,1)S(1)}, bf16[5,2,256,256]{3,2,1,0:T(8,128)(2,1)}, u32[]{:S(2)}) %copy-start) | copy-done | bytes 1310744
  2.7 0.0 copy-start.1
  2.7 1.2 %copy-done.1 = f32[2,2,256,256]{3,2,1,0:T(8,128)S(1)} copy-done((f32[2,2,256,256]{3,2,1,0:T(8,128)S(1)}, f32[2,2,256,256]{3,2,1,0:T(8,128)}, u32[]{:S(2)}) %copy-start.1) | copy-done | bytes 1048600
  3.9 0.0 copy-start.2
  3.9 1.0 %copy-done.2 = f32[2,256,256]{2,1,0:T(8,128)S(1)} copy-done((f32[2,256,256]{2,1,0:T(8,128)S(1)}, f32[2,256,256]{2,1,0:T(8,128)}, u32[]{:S(2)}) %copy-start.2) | copy-done | bytes 524312
  5.0 0.0 copy-start.3
  5.0 1.0 %copy-done.3 = f32[1,1,2,256,256]{4,3,2,1,0:T(8,128)S(1)} copy-done((f32[1,1,2,256,256]{4,3,2,1,0:T(8,128)S(1)}, f32[1,1,2,256,256]{4,3,2,1,0:T(8,128)}, u32[]{:S(2)}) %copy-start.3) | copy-done | bytes 524312
  6.0 0.0 copy-start.4
  6.0 0.9 %copy-done.4 = bf16[256,256]{1,0:T(8,128)(2,1)S(1)} copy-done((bf16[256,256]{1,0:T(8,128)(2,1)S(1)}, bf16[256,256]{1,0:T(8,128)(2,1)}, u32[]{:S(2)}) %copy-start.4) | copy-done | bytes 131096
  6.9 61.9 %step.1 = (f32[4,256,256]{2,1,0:T(8,128)S(1)}, f32[2,256,256]{2,1,0:T(8,128)S(1)}) custom-call(s32[4]{0:T(128)S(1)} %reshape.16.pos_ref, f32[4,256,256]{2,1,0:T(8,128)S(1)} %bitcast.4, f32[2,256,256]{2,1,0:T(8,128)S(1)} %copy-done.2, f32[2,256,256]{2,1,0:T(8,128)S(1)} %bitcast.5, bf16[5,2,256,256]{3,2,1,0:T(8,128)(2,1)S(1)} %copy-done, ...), custom_call_target="tpu_custom_call" | custom-call | tf_op jit(solution)/shard_map/step/pallas_call | solution.py:605
  68.8 1.0 %copy.10 = f32[2,2,256,256]{3,2,1,0:T(8,128)} copy(f32[2,2,256,256]{3,2,1,0:T(8,128)S(1)} %bitcast.3) | data formatting | bytes 2097152
  69.8 0.8 %copy.11 = f32[2,256,256]{2,1,0:T(8,128)} copy(f32[2,256,256]{2,1,0:T(8,128)S(1)} %get-tuple-element.9) | data formatting | bytes 1048576
Async XLA Ops:
  1.4 1.3 %copy-start = (bf16[5,2,256,256]{3,2,1,0:T(8,128)(2,1)S(1)}, bf16[5,2,256,256]{3,2,1,0:T(8,128)(2,1)}, u32[]{:S(2)}) copy-start(bf16[5,2,256,256]{3,2,1,0:T(8,128)(2,1)} %constant.4.clone.table_in) | copy-start | bytes 3932164
  2.7 1.2 %copy-start.1 = (f32[2,2,256,256]{3,2,1,0:T(8,128)S(1)}, f32[2,2,256,256]{3,2,1,0:T(8,128)}, u32[]{:S(2)}) copy-start(f32[2,2,256,256]{3,2,1,0:T(8,128)} %param.6) | copy-start | bytes 3145732
  3.9 1.0 %copy-start.2 = (f32[2,256,256]{2,1,0:T(8,128)S(1)}, f32[2,256,256]{2,1,0:T(8,128)}, u32[]{:S(2)}) copy-start(f32[2,256,256]{2,1,0:T(8,128)} %probe_in.1) | copy-start | bytes 1572868
  5.0 1.0 %copy-start.3 = (f32[1,1,2,256,256]{4,3,2,1,0:T(8,128)S(1)}, f32[1,1,2,256,256]{4,3,2,1,0:T(8,128)}, u32[]{:S(2)}) copy-start(f32[1,1,2,256,256]{4,3,2,1,0:T(8,128)} %param.9) | copy-start | bytes 1572868
  6.0 0.9 %copy-start.4 = (bf16[256,256]{1,0:T(8,128)(2,1)S(1)}, bf16[256,256]{1,0:T(8,128)(2,1)}, u32[]{:S(2)}) copy-start(bf16[256,256]{1,0:T(8,128)(2,1)} %constant.5.clone.perm_in) | copy-start | bytes 393220

commit v3 on v2

--- a/solution.py
+++ b/solution.py
@@ -15,7 +15,6 @@
 AROUND = ((-1, 0), (1, 0), (0, -1), (0, 1), (-1, -1), (-1, 1), (1, -1), (1, 1))
 CORES = 2
 NYX = (4, 4)
-SUBS = 2
 
 
 def split_of(matrix):
@@ -198,15 +197,15 @@
 
 def kernel(
     rows, cols, nyx,
-    pos_ref, obj_ref, probe_in, meas_in, table_in, perm_in,
+    pos_in, obj_ref, probe_in, meas_in, table_in, perm_in,
     obj_out, probe_out,
-    probe_ref, meas_ref, w_ref, perm_ref,
+    pos_ref, probe_ref, meas_ref, w_ref, perm_ref,
     win, pl_buf, pr_buf, hl, hr,
     cut, mid, pad, seen,
-    grad, gl, gr, gp_ref, fresh,
+    grad, gl, gr, gp_ref,
     theirs, ours, slots, mine, zslots, zpeak, xpeak, ppeak, total_ref,
     rt, rb, rl, rr, corners,
-    load_sem, store_sem,
+    load_sem,
     send_halo, recv_halo, send_rim, recv_rim, send_pair, recv_pair, send_xy, recv_xy, send_z, recv_z,
     send_zm, recv_zm, send_xm, recv_xm, send_all, recv_all, send_back, recv_back, send_pm, recv_pm,
 ):
@@ -217,7 +216,7 @@
     nxy = ny * nx
     nzl = cols // nxy
     nz = nzl * (rows // CORES)
-    step = n // nxy // SUBS
+    step = n // nxy
     r, c = place_of()
     core, zh = lax.rem(r, CORES), lax.div(r, CORES)
     zl, here = lax.div(c, nxy), lax.rem(c, nxy)
@@ -226,29 +225,19 @@
     partner = (zh * CORES + 1 - core, c)
 
     def peer(d):
-        oy, ox = lax.div(d, nx), lax.rem(d, nx)
-        q = lax.rem(y + oy, ny) * nx + lax.rem(x + ox, nx)
+        q = lax.rem(y + d // nx, ny) * nx + lax.rem(x + d % nx, nx)
         return q, (r, zl * nxy + q)
-
-    def source_of(d):
-        oy, ox = lax.div(d, nx), lax.rem(d, nx)
-        return lax.rem(y + ny - oy, ny) * nx + lax.rem(x + nx - ox, nx)
 
     def zpeer(d):
         k = lax.rem(z + d, nz)
         return lax.div(k, nzl) * CORES + core, lax.rem(k, nzl) * nxy + here
 
-    def each(count, body, low=0):
-        def go(i, carry):
-            body(count - 1 - i)
-            return carry
-
-        lax.fori_loop(0, count - low, go, 0)
+    far = sorted(range(1, nz), key=lambda d: -min(d, nz - d))
 
     around = neighbours(rows, cols)
     extra = [partner]
-    extra += [peer(jnp.int32(d))[1] for d in range(1, nxy)]
-    extra += [zpeer(jnp.int32(d)) for d in range(1, nz)]
+    extra += [peer(d)[1] for d in range(1, nxy)]
+    extra += [zpeer(d) for d in range(1, nz)]
     greet(around, extra)
 
     inner = pl.ds(RIM, n)
@@ -259,6 +248,7 @@
         (perm_in, perm_ref),
         (probe_in, probe_ref),
         (table_in, w_ref),
+        (pos_in, pos_ref),
     ]
     loads = [pltpu.make_async_copy(a, b, load_sem.at[i]) for i, (a, b) in enumerate(loads)]
     for load in loads:
@@ -313,12 +303,13 @@
         )
     loads[4].wait()
     loads[5].wait()
+    loads[6].wait()
     finish_rims(*halo)
     for q in range(4):
         win[q, 0] = pltpu.roll(hl[...], (96 - 32 * q) % 128, 1)
         win[q, 3] = pltpu.roll(hr[...], (128 - 32 * q) % 128, 1) if q else hr[...]
 
-    offs = [(pos_ref[2 * p], pos_ref[2 * p + 1]) for p in range(npos)]
+    offs = [(pos_ref[0, 0, p, 0], pos_ref[0, 0, p, 1]) for p in range(npos)]
     lane = lax.broadcasted_iota(jnp.int32, (RIM, 128), 1)
 
     def cut_rows(i, carry):
@@ -373,23 +364,18 @@
             gp_ref[0] += ar * er + ai * ei
             gp_ref[1] += ar * ei - ai * er
 
-    def band(q, s):
-        return rows_at((q * SUBS + s) * step, step)
-
-    def pair(s, d):
-        at = band(peer(d)[0], s)
-        return remote(
-            gp_ref.at[1 - core, at, :], theirs.at[at, :], send_pair.at[s, d], recv_pair.at[s, d], partner
-        )
-
-    def spread(s, d):
-        q, where = peer(d)
-        return remote(
-            ours.at[band(q, s), :], slots.at[s, d], send_xy.at[s, d], recv_xy.at[s, d], where
-        )
-
-    for s in range(SUBS):
-        each(nxy, lambda d, s=s: pair(s, d).start())
+    def band(q):
+        return rows_at(q * step, step)
+
+    def stripe(row):
+        return rows_at(row * step * nx, step * nx)
+
+    def pair(oy):
+        at = stripe(lax.rem(y + oy, ny))
+        return at, remote(gp_ref.at[1 - core, at, :], theirs.at[at, :], send_pair, recv_pair.at[oy], partner)
+
+    for oy in reversed(range(ny)):
+        pair(oy)[1].start()
 
     quarter = lax.div(lane, 32)
 
@@ -417,20 +403,17 @@
             ends.append((sums[0], sums[3]))
         gr[to, :], gl[to, :] = pack_sides(lambda q: ends[q][1], lambda q: ends[q][0], quarter)
 
-    def pass_on(s, d):
-        at = band(peer(d)[0], s)
-        pair(s, d).wait_recv()
+    for oy in reversed(range(ny)):
+        at, copy = pair(oy)
+        copy.wait_recv()
         ours[at, :] = gp_ref[core, at, :] + theirs[at, :]
-
-    def pass_and_send(s, d):
-        pass_on(s, d)
-        spread(s, d).start()
-
-    for s in range(SUBS):
-        each(nxy, lambda d, s=s: pass_and_send(s, d), 1)
-        pass_on(s, jnp.int32(0))
-
-    each(n // RIM + 2, place)
+        for ox in reversed(range(nx)):
+            d = oy * nx + ox
+            if d:
+                q, where = peer(d)
+                remote(ours.at[band(q), :], slots.at[d], send_xy, recv_xy, where).start()
+
+    lax.fori_loop(0, n // RIM + 2, lambda i, carry: (place(i), carry)[1], 0)
     rims = (
         around,
         [
@@ -443,20 +426,20 @@
     )
     swap_rims(*rims)
 
-    def to_z(s, d):
-        return remote(mine.at[s], zslots.at[s, z], send_z.at[s, d], recv_z.at[s, d], zpeer(d))
-
-    def peak_to_z(d):
-        return remote(zpeak.at[z], zpeak.at[z], send_zm.at[d], recv_zm.at[d], zpeer(d))
-
-    for s in range(SUBS):
-        each(nxy, lambda d, s=s: spread(s, d).wait_recv(), 1)
-        acc = ours[band(here, s), :]
-        for d in range(1, nxy):
-            acc = acc + slots[s, d]
-        mine[s] = acc
-        zslots[s, pl.ds(z, 1)] = acc[None]
-        each(nz, lambda d, s=s: to_z(s, d).start(), 1)
+    def landed(ref, sem):
+        remote(ref, ref, sem, sem, partner).wait_recv()
+
+    def left(ref, sem):
+        remote(ref, ref, sem, sem, partner).wait_send()
+
+    landed(slots.at[pl.ds(1, nxy - 1)], recv_xy)
+    acc = ours[band(here), :]
+    for d in range(1, nxy):
+        acc = acc + slots[d]
+    mine[...] = acc
+    zslots[pl.ds(z, 1)] = acc[None]
+    for d in far:
+        remote(mine, zslots.at[z], send_z, recv_z, zpeer(d)).start()
 
     finish_rims(*rims)
     first, final = lane < 32, lane >= 96
@@ -489,53 +472,43 @@
     peak = jnp.maximum(rows_of(0, 0, rt), rows_of(blocks - 1, 2, rb))
     peak = lax.fori_loop(1, blocks - 1, lambda i, m: jnp.maximum(m, rows_of(i, None, None)), peak)
     zpeak[pl.ds(z, 1)] = peak[None]
-    each(nz, lambda d: peak_to_z(d).start(), 1)
-
-    def to_all(s, d):
-        block = total_ref.at[core, band(here, s), :]
-        return remote(block, block, send_all.at[s, d], recv_all.at[s, d], peer(d)[1])
-
-    def peak_to_all(d):
-        return remote(xpeak.at[0], xpeak.at[d], send_xm.at[d], recv_xm.at[d], peer(d)[1])
-
-    def back(s, d):
-        block = total_ref.at[core, band(source_of(d), s), :]
-        return remote(block, block, send_back.at[s, d], recv_back.at[s, d], partner)
-
-    for s in range(SUBS):
-        each(nz, lambda d, s=s: to_z(s, d).wait_recv(), 1)
-        acc = zslots[s, 0]
-        for k in range(1, nz):
-            acc = acc + zslots[s, k]
-        total_ref[pl.ds(core, 1), band(here, s), :] = acc[None]
-        each(nxy, lambda d, s=s: to_all(s, d).start(), 1)
-        back(s, jnp.int32(0)).start()
-
-    each(nz, lambda d: peak_to_z(d).wait_recv(), 1)
+    for d in far:
+        remote(zpeak.at[z], zpeak.at[z], send_zm, recv_zm, zpeer(d)).start()
+
+    landed(zslots.at[pl.ds(0, nz - 1)], recv_z)
+    acc = zslots[0]
+    for k in range(1, nz):
+        acc = acc + zslots[k]
+    total_ref[pl.ds(core, 1), band(here), :] = acc[None]
+    block = total_ref.at[core, band(here), :]
+    for d in reversed(range(1, nxy)):
+        remote(block, block, send_all, recv_all.at[d // nx], peer(d)[1]).start()
+
+    landed(zpeak.at[pl.ds(0, nz - 1)], recv_zm)
     peak = zpeak[0]
     for k in range(1, nz):
         peak = jnp.maximum(peak, zpeak[k])
     xpeak[0] = peak
-    each(nxy, lambda d: peak_to_all(d).start(), 1)
-
-    def arrived(s, d):
-        block = total_ref.at[core, band(source_of(d), s), :]
-        remote(block, block, send_all.at[s, d], recv_all.at[s, d], partner).wait_recv()
-        back(s, d).start()
-
-    def forward(s):
-        lax.fori_loop(1, nxy, lambda d, carry: (arrived(s, d), carry)[1], 0)
-
-    for s in range(SUBS - 1):
-        forward(s)
-    each(nxy, lambda d: peak_to_all(d).wait_recv(), 1)
+    for d in reversed(range(1, nxy)):
+        remote(xpeak.at[0], xpeak.at[d], send_xm, recv_xm, peer(d)[1]).start()
+
+    def forward(oy):
+        at = stripe(lax.rem(y + ny - oy, ny))
+        block = total_ref.at[core, at, :]
+        count = nx - 1 if oy == 0 else nx
+        landed(total_ref.at[core, pl.ds(0, count * step), :], recv_all.at[oy])
+        remote(block, block, send_back, recv_back, partner).start()
+
+    forward(0)
+    landed(xpeak.at[pl.ds(1, nxy - 1)], recv_xm)
     peak = xpeak[0]
     for d in range(1, nxy):
         peak = jnp.maximum(peak, xpeak[d])
     ppeak[0] = peak
     last = remote(ppeak.at[0], ppeak.at[1], send_pm, recv_pm, partner)
     last.start()
-    forward(SUBS - 1)
+    for oy in range(1, ny):
+        forward(oy)
     last.wait()
 
     largest = jnp.max(jnp.maximum(ppeak[0], ppeak[1]), axis=(0, 1), keepdims=True)
@@ -545,37 +518,21 @@
         at = rows_at(i * RIM + RIM, RIM)
         for q in range(4):
             for t in (0, 1):
-                grad[q, t, at, :] = win[q, t + 1, at, :] - scale * grad[q, t, at, :]
+                obj_out[q, rows_at(i * RIM, RIM), 128 * t : 128 * t + 128] = (
+                    win[q, t + 1, at, :] - scale * grad[q, t, at, :]
+                )
         return carry
 
     lax.fori_loop(0, blocks, next_rows, 0)
-    stores = [
-        pltpu.make_async_copy(grad.at[:, t, inner, :], obj_out.at[:, :, pl.ds(128 * t, 128)], store_sem.at[t])
-        for t in (0, 1)
-    ]
-    for store in stores:
-        store.start()
-
-    def drain(s, d):
-        pair(s, d).wait_send()
-        back(s, d).wait()
-
-    def drain_xy(s, d):
-        spread(s, d).wait_send()
-        to_all(s, d).wait_send()
-
-    for s in range(SUBS):
-        each(nxy, lambda d, s=s: drain(s, d))
-    fresh[...] = probe_ref[...] - (2.0 / (rows * cols)) * total_ref[...]
-    stores.append(pltpu.make_async_copy(fresh, probe_out, store_sem.at[2]))
-    stores[2].start()
-    for s in range(SUBS):
-        each(nxy, lambda d, s=s: drain_xy(s, d), 1)
-        each(nz, lambda d, s=s: to_z(s, d).wait_send(), 1)
-    each(nxy, lambda d: peak_to_all(d).wait_send(), 1)
-    each(nz, lambda d: peak_to_z(d).wait_send(), 1)
-    for store in stores:
-        store.wait()
+    landed(total_ref.at[core], recv_back)
+    probe_out[...] = probe_ref[...] - (2.0 / (rows * cols)) * total_ref[...]
+    left(total_ref.at[core], send_back)
+    left(total_ref.at[core], send_pair)
+    left(slots.at[pl.ds(1, nxy - 1)], send_xy)
+    left(slots.at[pl.ds(1, nxy - 1)], send_all)
+    left(zslots.at[pl.ds(0, nz - 1)], send_z)
+    left(zpeak.at[pl.ds(0, nz - 1)], send_zm)
+    left(xpeak.at[pl.ds(1, nxy - 1)], send_xm)
 
 
 def local(rows, cols, nyx, table, perm, object_in, probe_in, positions, intensity):
@@ -583,38 +540,44 @@
     npos = positions.shape[2]
     f32 = jnp.float32
     hbm = pl.BlockSpec(memory_space=pltpu.HBM)
-    smem = pl.BlockSpec(memory_space=pltpu.SMEM)
+    vmem = pl.BlockSpec(memory_space=pltpu.VMEM)
     dma = pltpu.SemaphoreType.DMA
     nxy = nyx[0] * nyx[1]
     nz = rows * cols // (CORES * nxy)
-    step = n // nxy // SUBS
+    step = n // nxy
     wide = n + 2 * RIM
     buffers = [
         (2, n, n), (npos, n, n), table.shape, perm.shape,
         (4, 4, wide, 128), (n, 128), (n, 128), (wide, 128), (wide, 128),
         (npos, 4, 2, n, 128), (npos, 2, n, n), (npos, 4, 2, n + 128, 128), (npos, 2, n, 128),
-        (4, 2, wide, 128), (wide, 128), (wide, 128), (2, n, n), (2, n, n),
-        (n, n), (n, n), (SUBS, nxy, step, n), (SUBS, step, n), (SUBS, nz, step, n),
+        (4, 2, wide, 128), (wide, 128), (wide, 128), (2, n, n),
+        (n, n), (n, n), (nxy, step, n), (step, n), (nz, step, n),
         (nz, 8, 128), (nxy, 8, 128), (2, 8, 128), (2, n, n),
         (4, 2, RIM, 128), (4, 2, RIM, 128), (n, 128), (n, 128), (4, RIM, 128),
     ]
-    scratch = [VMEM(shape, jnp.bfloat16 if i in (2, 3) else f32) for i, shape in enumerate(buffers)]
-    scratch += [dma((6,)), dma((3,)), dma((8,)), dma((8,)), dma((8,)), dma((8,))]
-    scratch += [dma((SUBS, nxy))] * 4 + [dma((SUBS, nz))] * 2 + [dma((nz,))] * 2 + [dma((nxy,))] * 2
-    scratch += [dma((SUBS, nxy))] * 4 + [dma, dma]
+    scratch = [pltpu.SMEM(positions.shape, jnp.int32)]
+    scratch += [VMEM(shape, jnp.bfloat16 if i in (2, 3) else f32) for i, shape in enumerate(buffers)]
+    scratch += [dma((7,)), dma((8,)), dma((8,)), dma((8,)), dma((8,))]
+    scratch += [dma, dma((nyx[0],)), dma, dma, dma, dma]
+    scratch += [dma] * 4 + [dma, dma((nyx[0],)), dma, dma, dma, dma]
     object_out, probe_out = pl.pallas_call(
         functools.partial(kernel, rows, cols, nyx),
         out_shape=(jax.ShapeDtypeStruct((4, n, n), f32), jax.ShapeDtypeStruct((2, n, n), f32)),
-        in_specs=[smem] + [hbm] * 5,
-        out_specs=(hbm, hbm),
+        in_specs=[hbm] * 6,
+        out_specs=(vmem, vmem),
         scratch_shapes=scratch,
         compiler_params=pltpu.CompilerParams(
-            collective_id=0, has_side_effects=True, vmem_limit_bytes=48 * 2**20
+            collective_id=0, has_side_effects=True, vmem_limit_bytes=28 * 2**20
         ),
         name="step",
     )(
-        positions.reshape(-1), object_in.reshape(4, n, n), probe_in, intensity.reshape(npos, n, n),
-        jnp.asarray(table), jnp.asarray(perm),
+        *(
+            pltpu.with_memory_space_constraint(a, pltpu.HBM)
+            for a in (
+                positions, object_in.reshape(4, n, n), probe_in, intensity.reshape(npos, n, n),
+                jnp.asarray(table), jnp.asarray(perm),
+            )
+        )
     )
     return object_out.reshape(object_in.shape), probe_out
 

time: 70.9 us -> 58.5 us (0.83)
  local copies, waits for them, and re-layouts: 8.05 us -> 1.77 us
  Pallas kernels: 61.9 us -> 56 us
    pallas_call x1, Pallas kernels: 61.9 us -> 56 us  [local(): pl.pallas_call(functools.partial(kernel, rows, cols, nyx), out_shape=(jax...]
    unnamed x12 -> x2, local copies, waits for them, and re-layouts: 7.29 us -> 1.77 us
    reshape x1 -> x0, local copies, waits for them, and re-layouts: 0.76 us -> none  [local(): positions.reshape(-1)]
where the time goes in v3:
time: 58.5 us; the launch traced here: 58.4 us
  Pallas kernels  56 us (96%)
  local copies, waits for them, and re-layouts  1.77 us (3%)
  between operations  0.64 us (1%)
    pallas_call x1, Pallas kernels, local(): pl.pallas_call(functools.partial(kernel, rows, cols, nyx), out_shape=(jax...  56 us
    unnamed x2, local copies, waits for them, and re-layouts  1.77 us

profile of v3, /device:TPU:1, one launch (start us, length us, event | category | flops | bytes accessed | tf_op | source)
XLA Modules:
  0.0 58.4 jit_solution(13753952790180503383)
XLA Ops:
  0.6 56.0 %step.1 = (f32[4,256,256]{2,1,0:T(8,128)S(1)}, f32[2,256,256]{2,1,0:T(8,128)S(1)}) custom-call(s32[1,1,2,2]{3,2,1,0:T(2,128)} %pos_in.1, f32[4,256,256]{2,1,0:T(8,128)} %bitcast.4, f32[2,256,256]{2,1,0:T(8,128)} %probe_in.1, f32[2,256,256]{2,1,0:T(8,128)} %bitcast.5, bf16[5,2,256,256]{3,2,1,0:T(8,128)(2,1)} %constant.4.clone.table_in, ...), custom_call_target="tpu_custom_call" | custom-call | tf_op jit(solution)/shard_map/step/pallas_call | solution.py:563
  56.7 1.0 %copy.10 = f32[2,2,256,256]{3,2,1,0:T(8,128)} copy(f32[2,2,256,256]{3,2,1,0:T(8,128)S(1)} %bitcast.3) | data formatting | bytes 2097152
  57.6 0.8 %copy.11 = f32[2,256,256]{2,1,0:T(8,128)} copy(f32[2,256,256]{2,1,0:T(8,128)S(1)} %get-tuple-element.9) | data formatting | bytes 1048576

commit v4 on v3

--- a/solution.py
+++ b/solution.py
@@ -166,10 +166,10 @@
     pl.semaphore_wait(pltpu.get_barrier_semaphore(), tall * wide - 1 + len(extra))
 
 
-def swap_rims(around, sources, targets, send_sem, recv_sem):
+def swap_rims(around, sources, targets, send_sem, recv_sem, wave):
     for d, (ok, where) in enumerate(around):
         o = opposite(d)
-        copy = remote(sources[d], targets[o], send_sem.at[d], recv_sem.at[o], where)
+        copy = remote(sources[d], targets[o], send_sem.at[wave, d], recv_sem.at[wave, o], where)
         pl.when(ok)(copy.start)
         target = targets[d]
 
@@ -178,20 +178,25 @@
             target[...] = jnp.zeros(target.shape, target.dtype)
 
 
-def finish_rims(around, sources, targets, send_sem, recv_sem):
+def finish_rims(around, sources, targets, send_sem, recv_sem, wave):
     for d, (ok, where) in enumerate(around):
-        pl.when(ok)(remote(sources[d], targets[d], send_sem.at[d], recv_sem.at[d], where).wait)
+        copy = remote(sources[d], targets[d], send_sem.at[wave, d], recv_sem.at[wave, d], where)
+        pl.when(ok)(copy.wait)
 
 
 def both(ref, *at):
     return jnp.concatenate([ref[(*at, 0)], ref[(*at, 1)]], 1)
 
 
+def turn(x, lanes):
+    return pltpu.roll(x, lanes % 128, 1) if lanes % 128 else x
+
+
 def pack_sides(first, last, quarter):
-    left, right = first(0), pltpu.roll(last(0), 32, 1)
-    for q in range(1, 4):
-        left = jnp.where(quarter == q, pltpu.roll(first(q), 32 * q, 1), left)
-        right = jnp.where(quarter == q, pltpu.roll(last(q), (32 * q + 32) % 128, 1), right)
+    left, right = first(0), turn(last(0), 32)
+    for k in range(1, 4):
+        left = jnp.where(quarter == k, turn(first(k), 32 * k), left)
+        right = jnp.where(quarter == k, turn(last(k), 32 * k + 32), right)
     return left, right
 
 
@@ -200,14 +205,14 @@
     pos_in, obj_ref, probe_in, meas_in, table_in, perm_in,
     obj_out, probe_out,
     pos_ref, probe_ref, meas_ref, w_ref, perm_ref,
-    win, pl_buf, pr_buf, hl, hr,
+    win_a, win_b, pl_buf, pr_buf, hl, hr, hc,
     cut, mid, pad, seen,
-    grad, gl, gr, gp_ref,
-    theirs, ours, slots, mine, zslots, zpeak, xpeak, ppeak, total_ref,
+    grad, gl, gr, gcl, gcr, gp_ref,
+    theirs, ours, slots, mine, zslots, zpeak, xpeak, total_ref,
     rt, rb, rl, rr, corners,
     load_sem,
     send_halo, recv_halo, send_rim, recv_rim, send_pair, recv_pair, send_xy, recv_xy, send_z, recv_z,
-    send_zm, recv_zm, send_xm, recv_xm, send_all, recv_all, send_back, recv_back, send_pm, recv_pm,
+    send_zm, recv_zm, send_xm, recv_xm, send_all, recv_all, send_back, recv_back,
 ):
     n = probe_ref.shape[-1]
     h = n // 2
@@ -232,18 +237,27 @@
         k = lax.rem(z + d, nz)
         return lax.div(k, nzl) * CORES + core, lax.rem(k, nzl) * nxy + here
 
+    def zother(d):
+        k = lax.rem(z + d, nz)
+        return lax.div(k, nzl) * CORES + 1 - core, lax.rem(k, nzl) * nxy + here
+
     far = sorted(range(1, nz), key=lambda d: -min(d, nz - d))
 
     around = neighbours(rows, cols)
     extra = [partner]
     extra += [peer(d)[1] for d in range(1, nxy)]
     extra += [zpeer(d) for d in range(1, nz)]
+    extra += [zother(d) for d in range(1, nz)]
     greet(around, extra)
 
+    win = (win_a, win_b)
     inner = pl.ds(RIM, n)
     loads = [
-        (obj_ref.at[:, :, pl.ds(0, 128)], win.at[:, 1, inner, :]),
-        (obj_ref.at[:, :, pl.ds(128, 128)], win.at[:, 2, inner, :]),
+        (obj_ref.at[pl.ds(2 * l, 2), :, pl.ds(128 * t, 128)], win[l].at[:, t + 1, inner, :])
+        for l in (0, 1)
+        for t in (0, 1)
+    ]
+    loads += [
         (meas_in, meas_ref),
         (perm_in, perm_ref),
         (probe_in, probe_ref),
@@ -253,31 +267,37 @@
     loads = [pltpu.make_async_copy(a, b, load_sem.at[i]) for i, (a, b) in enumerate(loads)]
     for load in loads:
         load.start()
-    loads[0].wait()
-    loads[1].wait()
-    quarter = lax.div(lax.broadcasted_iota(jnp.int32, (n, 128), 1), 32)
-    pl_buf[...], pr_buf[...] = pack_sides(
-        lambda q: win[q, 1, RIM : RIM + n, :], lambda q: win[q, 2, RIM : RIM + n, :], quarter
-    )
+    quarter = lax.div(lax.broadcasted_iota(jnp.int32, (h, 128), 1), 32)
+    for l in (0, 1):
+        loads[2 * l].wait()
+        loads[2 * l + 1].wait()
+
+        def piece(t, k, l=l):
+            return win[l][k % 2, t, RIM + h * (k // 2) : RIM + h * (k // 2) + h, :]
+
+        pl_buf[l], pr_buf[l] = pack_sides(lambda k: piece(1, k), lambda k: piece(2, k), quarter)
     await_greetings(rows, cols, extra)
 
     ups, tops = pl.ds(0, RIM), pl.ds(RIM, RIM)
     lows, downs = pl.ds(n, RIM), pl.ds(n + RIM, RIM)
-    lo, hi = pl.ds(0, RIM), pl.ds(n - RIM, RIM)
-    halo = (
-        around,
-        [
-            win.at[:, 1:3, tops, :], win.at[:, 1:3, lows, :], pl_buf, pr_buf,
-            pl_buf.at[lo, :], pr_buf.at[lo, :], pl_buf.at[hi, :], pr_buf.at[hi, :],
-        ],
-        [
-            win.at[:, 1:3, ups, :], win.at[:, 1:3, downs, :], hl.at[inner, :], hr.at[inner, :],
-            hl.at[ups, :], hr.at[ups, :], hl.at[downs, :], hr.at[downs, :],
-        ],
-        send_halo,
-        recv_halo,
-    )
-    swap_rims(*halo)
+    lo, hi = pl.ds(0, RIM), pl.ds(h - RIM, RIM)
+    halo = [
+        (
+            around,
+            [
+                win[l].at[:, 1:3, tops, :], win[l].at[:, 1:3, lows, :], pl_buf.at[l], pr_buf.at[l],
+                pl_buf.at[l, lo, :], pr_buf.at[l, lo, :], pl_buf.at[l, hi, :], pr_buf.at[l, hi, :],
+            ],
+            [win[l].at[:, 1:3, ups, :], win[l].at[:, 1:3, downs, :], hl.at[l], hr.at[l]]
+            + [hc.at[l, k] for k in range(4)],
+            send_halo,
+            recv_halo,
+            l,
+        )
+        for l in (0, 1)
+    ]
+    for l in (0, 1):
+        swap_rims(*halo[l])
 
     zeros = jnp.zeros((64, 128), jnp.float32)
     for p in range(npos):
@@ -285,8 +305,8 @@
             for t in (0, 1):
                 pad[p, q, t, 0:64, :] = zeros
                 pad[p, q, t, 64 + n :, :] = zeros
-    loads[2].wait()
-    loads[3].wait()
+    loads[4].wait()
+    loads[5].wait()
     for p in range(npos):
         for t in (0, 1):
             seen[p, t] = meas_ref[p, :, 128 * t : 128 * t + 128]
@@ -301,42 +321,103 @@
         meas_ref[p] = dot(
             jnp.concatenate([mh, ml], 1), jnp.concatenate([perm_ref[...], perm_ref[...]], 0)
         )
-    loads[4].wait()
-    loads[5].wait()
-    loads[6].wait()
-    finish_rims(*halo)
-    for q in range(4):
-        win[q, 0] = pltpu.roll(hl[...], (96 - 32 * q) % 128, 1)
-        win[q, 3] = pltpu.roll(hr[...], (128 - 32 * q) % 128, 1) if q else hr[...]
-
+    for load in loads[6:]:
+        load.wait()
     offs = [(pos_ref[0, 0, p, 0], pos_ref[0, 0, p, 1]) for p in range(npos)]
     lane = lax.broadcasted_iota(jnp.int32, (RIM, 128), 1)
 
-    def cut_rows(i, carry):
-        for p in range(npos):
-            dy, dx = offs[p]
-            shift = lax.rem(128 - dx, 128)
-            high, low = lane >= 128 - dx, lane < -dx
-            for q in range(4):
-                at = pl.ds(RIM + dy + i * RIM, RIM)
-                t0, t1, t2, t3 = [pltpu.roll(win[q, t, at, :], shift, 1) for t in range(4)]
-                to = rows_at(i * RIM, RIM)
-                cut[p, q, 0, to, :] = jnp.where(high, t2, jnp.where(low, t0, t1))
-                cut[p, q, 1, to, :] = jnp.where(high, t3, jnp.where(low, t1, t2))
-        return carry
-
-    lax.fori_loop(0, n // RIM, cut_rows, 0)
+    def cut_slice(l):
+        finish_rims(*halo[l])
+        for a in (0, 1):
+            for k in (0, 1):
+                at = slice(RIM + h * k, RIM + h * k + h)
+                win[l][a, 0, at, :] = turn(hl[l], 96 - 32 * (2 * k + a))
+                win[l][a, 3, at, :] = turn(hr[l], -32 * (2 * k + a))
+            win[l][a, 0, 0:RIM, :] = turn(hc[l, 0], 96 - 32 * (2 + a))
+            win[l][a, 3, 0:RIM, :] = turn(hc[l, 1], -32 * (2 + a))
+            win[l][a, 0, RIM + n :, :] = turn(hc[l, 2], 96 - 32 * a)
+            win[l][a, 3, RIM + n :, :] = turn(hc[l, 3], -32 * a)
+
+        def cut_rows(i, carry):
+            for p in range(npos):
+                dy, dx = offs[p]
+                shift = lax.rem(128 - dx, 128)
+                high, low = lane >= 128 - dx, lane < -dx
+                for a in (0, 1):
+                    at = pl.ds(RIM + dy + i * RIM, RIM)
+                    t0, t1, t2, t3 = [pltpu.roll(win[l][a, t, at, :], shift, 1) for t in range(4)]
+                    to = rows_at(i * RIM, RIM)
+                    cut[p, 2 * l + a, 0, to, :] = jnp.where(high, t2, jnp.where(low, t0, t1))
+                    cut[p, 2 * l + a, 1, to, :] = jnp.where(high, t3, jnp.where(low, t1, t2))
+            return carry
+
+        lax.fori_loop(0, n // RIM, cut_rows, 0)
 
     def keep(p, q, value):
         pad[p, q, 0, 64 : 64 + n, :] = value[:, :128]
         pad[p, q, 1, 64 : 64 + n, :] = value[:, 128:]
 
+    quarter = lax.div(lane, 32)
+
+    def window_rows(l, a, start):
+        sums = None
+        for p in range(npos):
+            dy, dx = offs[p]
+            shift = lax.rem(128 + dx, 128)
+            low, high = lane < dx, lane >= 128 + dx
+            at = pl.ds(RIM - dy + start, RIM)
+            u, v = (pltpu.roll(pad[p, 2 * l + a, t, at, :], shift, 1) for t in (0, 1))
+            o = jnp.zeros_like(u)
+            got = [
+                jnp.where(high, u, o),
+                jnp.where(low, o, jnp.where(high, v, u)),
+                jnp.where(low, u, jnp.where(high, o, v)),
+                jnp.where(low, v, o),
+            ]
+            sums = got if sums is None else [e + f for e, f in zip(sums, got)]
+        return sums
+
+    def place(l, starts):
+        got = [window_rows(l, a, start) for start in starts for a in (0, 1)]
+        for k, four in enumerate(got):
+            to = rows_at(starts[k // 2], RIM)
+            grad[2 * l + k % 2, 0, to, :] = four[1]
+            grad[2 * l + k % 2, 1, to, :] = four[2]
+        right, left = pack_sides(lambda k: got[k][3], lambda k: got[k][0], quarter)
+        return left, right
+
+    def place_slice(l):
+        gcl[l], gcr[l] = place(l, (0, RIM + n))
+
+        def go(i, carry):
+            to = rows_at(i * RIM, RIM)
+            gl[l, to, :], gr[l, to, :] = place(l, (i * RIM + RIM, i * RIM + RIM + h))
+            return carry
+
+        lax.fori_loop(0, h // RIM, go, 0)
+
+    rims = [
+        (
+            around,
+            [grad.at[pl.ds(2 * l, 2), :, ups, :], grad.at[pl.ds(2 * l, 2), :, downs, :], gl.at[l], gr.at[l]]
+            + [gcl.at[l], gcr.at[l]] * 2,
+            [rt.at[l], rb.at[l], rl.at[l], rr.at[l]] + [corners.at[l, k] for k in range(4)],
+            send_rim,
+            recv_rim,
+            l,
+        )
+        for l in (0, 1)
+    ]
+
+    cut_slice(0)
     for p in range(npos):
         pr, pi = probe_ref[0], probe_ref[1]
         ar, ai = both(cut, p, 0), both(cut, p, 1)
         re, im = sandwich(fold(pr * ar - pi * ai), fold(pr * ai + pi * ar), w_ref, *PROP)
-        qr, qi = unfold(re), unfold(im)
-        mid[p, 0], mid[p, 1] = qr, qi
+        mid[p, 0], mid[p, 1] = unfold(re), unfold(im)
+    cut_slice(1)
+    for p in range(npos):
+        qr, qi = mid[p, 0], mid[p, 1]
         br, bi = both(cut, p, 2), both(cut, p, 3)
         re, im = sandwich(fold(qr * br - qi * bi), fold(qr * bi + qi * br), w_ref, *FORWARD)
         for i in (0, 1):
@@ -351,7 +432,11 @@
         keep(p, 2, qr * hr_ + qi * hi_)
         keep(p, 3, qr * hi_ - qi * hr_)
         br, bi = both(cut, p, 2), both(cut, p, 3)
-        re, im = sandwich(fold(br * hr_ + bi * hi_), fold(br * hi_ - bi * hr_), w_ref, *PROP_CONJ)
+        mid[p, 0], mid[p, 1] = br * hr_ + bi * hi_, br * hi_ - bi * hr_
+    place_slice(1)
+    swap_rims(*rims[1])
+    for p in range(npos):
+        re, im = sandwich(fold(mid[p, 0]), fold(mid[p, 1]), w_ref, *PROP_CONJ)
         er, ei = unfold(re), unfold(im)
         pr, pi = probe_ref[0], probe_ref[1]
         keep(p, 0, pr * er + pi * ei)
@@ -377,31 +462,8 @@
     for oy in reversed(range(ny)):
         pair(oy)[1].start()
 
-    quarter = lax.div(lane, 32)
-
-    def place(i):
-        to = rows_at(i * RIM, RIM)
-        ends = []
-        for q in range(4):
-            sums = None
-            for p in range(npos):
-                dy, dx = offs[p]
-                shift = lax.rem(128 + dx, 128)
-                low, high = lane < dx, lane >= 128 + dx
-                at = pl.ds(RIM - dy + i * RIM, RIM)
-                a, b = (pltpu.roll(pad[p, q, t, at, :], shift, 1) for t in (0, 1))
-                o = jnp.zeros_like(a)
-                got = [
-                    jnp.where(high, a, o),
-                    jnp.where(low, o, jnp.where(high, b, a)),
-                    jnp.where(low, a, jnp.where(high, o, b)),
-                    jnp.where(low, b, o),
-                ]
-                sums = got if sums is None else [u + v for u, v in zip(sums, got)]
-            grad[q, 0, to, :] = sums[1]
-            grad[q, 1, to, :] = sums[2]
-            ends.append((sums[0], sums[3]))
-        gr[to, :], gl[to, :] = pack_sides(lambda q: ends[q][1], lambda q: ends[q][0], quarter)
+    place_slice(0)
+    swap_rims(*rims[0])
 
     for oy in reversed(range(ny)):
         at, copy = pair(oy)
@@ -413,19 +475,6 @@
                 q, where = peer(d)
                 remote(ours.at[band(q), :], slots.at[d], send_xy, recv_xy, where).start()
 
-    lax.fori_loop(0, n // RIM + 2, lambda i, carry: (place(i), carry)[1], 0)
-    rims = (
-        around,
-        [
-            grad.at[:, :, ups, :], grad.at[:, :, downs, :], gl.at[inner, :], gr.at[inner, :],
-            gl.at[ups, :], gr.at[ups, :], gl.at[downs, :], gr.at[downs, :],
-        ],
-        [rt, rb, rl, rr, corners.at[0], corners.at[1], corners.at[2], corners.at[3]],
-        send_rim,
-        recv_rim,
-    )
-    swap_rims(*rims)
-
     def landed(ref, sem):
         remote(ref, ref, sem, sem, partner).wait_recv()
 
@@ -441,39 +490,49 @@
     for d in far:
         remote(mine, zslots.at[z], send_z, recv_z, zpeer(d)).start()
 
-    finish_rims(*rims)
     first, final = lane < 32, lane >= 96
-
-    def rows_of(i, up, low):
-        at, to = rows_at(i * RIM, RIM), rows_at(i * RIM + RIM, RIM)
-        zero = jnp.zeros((RIM, 128), jnp.float32)
-        lft, rgt = rl[at, :], rr[at, :]
-        if up is not None:
-            lft, rgt = lft + corners[up], rgt + corners[up + 1]
-        best = None
-        for l in (0, 1):
-            square = [None, None]
-            for q in (2 * l, 2 * l + 1):
-                ends = (
-                    jnp.where(first, pltpu.roll(lft, (128 - 32 * q) % 128, 1) if q else lft, zero),
-                    jnp.where(final, pltpu.roll(rgt, 96 - 32 * q, 1) if q < 3 else rgt, zero),
+    zero = jnp.zeros((RIM, 128), jnp.float32)
+
+    def rows_of(l, k, i):
+        at, to = rows_at(i * RIM, RIM), rows_at(h * k + i * RIM + RIM, RIM)
+        square = [None, None]
+        for a in (0, 1):
+            lane_of = 32 * (2 * k + a)
+            ends = (
+                jnp.where(first, turn(rl[l, at, :], -lane_of), zero),
+                jnp.where(final, turn(rr[l, at, :], 96 - lane_of), zero),
+            )
+            for t in (0, 1):
+                v = grad[2 * l + a, t, to, :] + ends[t]
+                grad[2 * l + a, t, to, :] = v
+                square[t] = v * v if square[t] is None else square[t] + v * v
+        best = jnp.maximum(square[0], square[1])
+        return functools.reduce(jnp.maximum, [best[8 * b : 8 * b + 8] for b in range(RIM // 8)])
+
+    def add_edges(l):
+        for edge, (strip, to, c) in enumerate(((rt, RIM, 0), (rb, n, 2))):
+            for a in (0, 1):
+                lane_of = 32 * (2 * (1 - edge) + a)
+                sides = (
+                    jnp.where(first, turn(corners[l, c], -lane_of), zero),
+                    jnp.where(final, turn(corners[l, c + 1], 96 - lane_of), zero),
                 )
                 for t in (0, 1):
-                    v = grad[q, t, to, :] + ends[t]
-                    if low is not None:
-                        v = v + low[q, t]
-                    grad[q, t, to, :] = v
-                    square[t] = v * v if square[t] is None else square[t] + v * v
-            for v in square:
-                best = v if best is None else jnp.maximum(best, v)
-        return functools.reduce(jnp.maximum, [best[8 * k : 8 * k + 8] for k in range(RIM // 8)])
-
-    blocks = n // RIM
-    peak = jnp.maximum(rows_of(0, 0, rt), rows_of(blocks - 1, 2, rb))
-    peak = lax.fori_loop(1, blocks - 1, lambda i, m: jnp.maximum(m, rows_of(i, None, None)), peak)
-    zpeak[pl.ds(z, 1)] = peak[None]
-    for d in far:
-        remote(zpeak.at[z], zpeak.at[z], send_zm, recv_zm, zpeer(d)).start()
+                    grad[2 * l + a, t, to : to + RIM, :] += strip[l, a, t] + sides[t]
+
+    def finish_slice(l):
+        finish_rims(*rims[l])
+        add_edges(l)
+        peak = jnp.zeros((8, 128), jnp.float32)
+        for k in (0, 1):
+            peak = lax.fori_loop(
+                0, h // RIM, lambda i, m, k=k: jnp.maximum(m, rows_of(l, k, i)), peak
+            )
+        return peak
+
+    xpeak[0] = jnp.maximum(finish_slice(1), finish_slice(0))
+    for d in reversed(range(1, nxy)):
+        remote(xpeak.at[0], xpeak.at[d], send_xm, recv_xm, peer(d)[1]).start()
 
     landed(zslots.at[pl.ds(0, nz - 1)], recv_z)
     acc = zslots[0]
@@ -484,13 +543,15 @@
     for d in reversed(range(1, nxy)):
         remote(block, block, send_all, recv_all.at[d // nx], peer(d)[1]).start()
 
-    landed(zpeak.at[pl.ds(0, nz - 1)], recv_zm)
-    peak = zpeak[0]
-    for k in range(1, nz):
-        peak = jnp.maximum(peak, zpeak[k])
-    xpeak[0] = peak
-    for d in reversed(range(1, nxy)):
-        remote(xpeak.at[0], xpeak.at[d], send_xm, recv_xm, peer(d)[1]).start()
+    landed(xpeak.at[pl.ds(1, nxy - 1)], recv_xm)
+    peak = xpeak[0]
+    for d in range(1, nxy):
+        peak = jnp.maximum(peak, xpeak[d])
+    zpeak[0] = peak
+    for d in far:
+        remote(zpeak.at[0], zpeak.at[d], send_zm, recv_zm, zpeer(d)).start()
+        remote(zpeak.at[0], zpeak.at[nz + d], send_zm, recv_zm, zother(d)).start()
+    remote(zpeak.at[0], zpeak.at[nz], send_zm, recv_zm, partner).start()
 
     def forward(oy):
         at = stripe(lax.rem(y + ny - oy, ny))
@@ -499,19 +560,14 @@
         landed(total_ref.at[core, pl.ds(0, count * step), :], recv_all.at[oy])
         remote(block, block, send_back, recv_back, partner).start()
 
-    forward(0)
-    landed(xpeak.at[pl.ds(1, nxy - 1)], recv_xm)
-    peak = xpeak[0]
-    for d in range(1, nxy):
-        peak = jnp.maximum(peak, xpeak[d])
-    ppeak[0] = peak
-    last = remote(ppeak.at[0], ppeak.at[1], send_pm, recv_pm, partner)
-    last.start()
-    for oy in range(1, ny):
+    for oy in range(ny):
         forward(oy)
-    last.wait()
-
-    largest = jnp.max(jnp.maximum(ppeak[0], ppeak[1]), axis=(0, 1), keepdims=True)
+    landed(zpeak.at[pl.ds(1, 2 * nz - 1)], recv_zm)
+    peak = zpeak[0]
+    for d in range(1, 2 * nz):
+        peak = jnp.maximum(peak, zpeak[d])
+
+    largest = jnp.max(peak, axis=(0, 1), keepdims=True)
     scale = jnp.broadcast_to(0.3 / (jnp.sqrt(largest) + 1e-06), (RIM, 128))
 
     def next_rows(i, carry):
@@ -519,11 +575,11 @@
         for q in range(4):
             for t in (0, 1):
                 obj_out[q, rows_at(i * RIM, RIM), 128 * t : 128 * t + 128] = (
-                    win[q, t + 1, at, :] - scale * grad[q, t, at, :]
+                    win[q // 2][q % 2, t + 1, at, :] - scale * grad[q, t, at, :]
                 )
         return carry
 
-    lax.fori_loop(0, blocks, next_rows, 0)
+    lax.fori_loop(0, n // RIM, next_rows, 0)
     landed(total_ref.at[core], recv_back)
     probe_out[...] = probe_ref[...] - (2.0 / (rows * cols)) * total_ref[...]
     left(total_ref.at[core], send_back)
@@ -531,7 +587,7 @@
     left(slots.at[pl.ds(1, nxy - 1)], send_xy)
     left(slots.at[pl.ds(1, nxy - 1)], send_all)
     left(zslots.at[pl.ds(0, nz - 1)], send_z)
-    left(zpeak.at[pl.ds(0, nz - 1)], send_zm)
+    left(zpeak.at[pl.ds(1, 2 * nz - 1)], send_zm)
     left(xpeak.at[pl.ds(1, nxy - 1)], send_xm)
 
 
@@ -548,18 +604,19 @@
     wide = n + 2 * RIM
     buffers = [
         (2, n, n), (npos, n, n), table.shape, perm.shape,
-        (4, 4, wide, 128), (n, 128), (n, 128), (wide, 128), (wide, 128),
+        (2, 4, wide, 128), (2, 4, wide, 128), (2, n // 2, 128), (2, n // 2, 128), (2, n // 2, 128), (2, n // 2, 128),
+        (2, 4, RIM, 128),
         (npos, 4, 2, n, 128), (npos, 2, n, n), (npos, 4, 2, n + 128, 128), (npos, 2, n, 128),
-        (4, 2, wide, 128), (wide, 128), (wide, 128), (2, n, n),
+        (4, 2, wide, 128), (2, n // 2, 128), (2, n // 2, 128), (2, RIM, 128), (2, RIM, 128), (2, n, n),
         (n, n), (n, n), (nxy, step, n), (step, n), (nz, step, n),
-        (nz, 8, 128), (nxy, 8, 128), (2, 8, 128), (2, n, n),
-        (4, 2, RIM, 128), (4, 2, RIM, 128), (n, 128), (n, 128), (4, RIM, 128),
+        (2 * nz, 8, 128), (nxy, 8, 128), (2, n, n),
+        (2, 2, 2, RIM, 128), (2, 2, 2, RIM, 128), (2, n // 2, 128), (2, n // 2, 128), (2, 4, RIM, 128),
     ]
     scratch = [pltpu.SMEM(positions.shape, jnp.int32)]
     scratch += [VMEM(shape, jnp.bfloat16 if i in (2, 3) else f32) for i, shape in enumerate(buffers)]
-    scratch += [dma((7,)), dma((8,)), dma((8,)), dma((8,)), dma((8,))]
+    scratch += [dma((9,)), dma((2, 8)), dma((2, 8)), dma((2, 8)), dma((2, 8))]
     scratch += [dma, dma((nyx[0],)), dma, dma, dma, dma]
-    scratch += [dma] * 4 + [dma, dma((nyx[0],)), dma, dma, dma, dma]
+    scratch += [dma] * 4 + [dma, dma((nyx[0],)), dma, dma]
     object_out, probe_out = pl.pallas_call(
         functools.partial(kernel, rows, cols, nyx),
         out_shape=(jax.ShapeDtypeStruct((4, n, n), f32), jax.ShapeDtypeStruct((2, n, n), f32)),

time: 58.5 us -> 54.4 us (0.930)
  Pallas kernels: 56 us -> 51.9 us
    pallas_call x1, Pallas kernels: 56 us -> 51.9 us  [local(): pl.pallas_call(functools.partial(kernel, rows, cols, nyx), out_shape=(jax...]
where the time goes in v4:
time: 54.4 us; the launch traced here: 54.3 us
  Pallas kernels  51.9 us (95%)
  local copies, waits for them, and re-layouts  1.77 us (3%)
  between operations  0.64 us (1%)
    pallas_call x1, Pallas kernels, local(): pl.pallas_call(functools.partial(kernel, rows, cols, nyx), out_shape=(jax...  51.9 us
    unnamed x2, local copies, waits for them, and re-layouts  1.77 us

profile of v4, /device:TPU:1, one launch (start us, length us, event | category | flops | bytes accessed | tf_op | source)
XLA Modules:
  0.0 54.3 jit_solution(5635783003652122766)
XLA Ops:
  0.6 51.9 %step.1 = (f32[4,256,256]{2,1,0:T(8,128)S(1)}, f32[2,256,256]{2,1,0:T(8,128)S(1)}) custom-call(s32[1,1,2,2]{3,2,1,0:T(2,128)} %pos_in.1, f32[4,256,256]{2,1,0:T(8,128)} %bitcast.4, f32[2,256,256]{2,1,0:T(8,128)} %probe_in.1, f32[2,256,256]{2,1,0:T(8,128)} %bitcast.5, bf16[5,2,256,256]{3,2,1,0:T(8,128)(2,1)} %constant.4.clone.table_in, ...), custom_call_target="tpu_custom_call" | custom-call | tf_op jit(solution)/shard_map/step/pallas_call | solution.py:620
  52.5 1.0 %copy.10 = f32[2,2,256,256]{3,2,1,0:T(8,128)} copy(f32[2,2,256,256]{3,2,1,0:T(8,128)S(1)} %bitcast.3) | data formatting | bytes 2097152
  53.5 0.8 %copy.11 = f32[2,256,256]{2,1,0:T(8,128)} copy(f32[2,256,256]{2,1,0:T(8,128)S(1)} %get-tuple-element.9) | data formatting | bytes 1048576

commit v5 on v4

--- a/solution.py
+++ b/solution.py
@@ -56,14 +56,14 @@
     return jnp.dot(a, b, preferred_element_type=jnp.float32)
 
 
-def times_right(x, w_ref, k):
-    high, low = parts(x)
+def times_right(split, w_ref, k):
+    high, low = split
     wh, wl = w_ref[k, 0], w_ref[k, 1]
     return dot(jnp.concatenate([high, low, high], 1), jnp.concatenate([wh, wh, wl], 0))
 
 
-def times_left(x, w_ref, k):
-    high, low = parts(x)
+def times_left(split, w_ref, k):
+    high, low = split
     wh, wl = w_ref[k, 0], w_ref[k, 1]
     return dot(jnp.concatenate([wh, wh, wl], 1), jnp.concatenate([high, low, high], 0))
 
@@ -84,28 +84,52 @@
 
 def sandwich(re, im, w_ref, right, left):
     h = re[0][0].shape[0]
-    out = [None, None]
+    split = []
+    for j in (0, 1):
+        first, second = (im, re) if right[j][1] else (re, im)
+        x = jnp.concatenate(
+            [jnp.concatenate([first[i][j], second[i][j]], 1) for i in (0, 1)], 0
+        )
+        split.append(parts(x))
+    yield
+    out = []
     for j in (0, 1):
         k, swap = right[j]
-        first, second = (im, re) if swap else (re, im)
-        x = jnp.concatenate(
-            [jnp.concatenate([first[i][j], second[i][j]], 1) for i in (0, 1)], 0
-        )
-        y = times_right(x, w_ref, k)
+        y = times_right(split[j], w_ref, k)
         a, b = y[:, :h], y[:, h:]
-        out[j] = (b, a) if swap else (a, b)
+        out.append((b, a) if swap else (a, b))
+    yield
+    split = []
+    for i in (0, 1):
+        rows = slice(i * h, (i + 1) * h)
+        r = jnp.concatenate([out[0][0][rows], out[1][0][rows]], 1)
+        m = jnp.concatenate([out[0][1][rows], out[1][1][rows]], 1)
+        split.append(parts(jnp.concatenate([m, r] if left[i][1] else [r, m], 0)))
+    yield
     res_re, res_im = [None, None], [None, None]
     for i in (0, 1):
         k, swap = left[i]
-        rows = slice(i * h, (i + 1) * h)
-        r = jnp.concatenate([out[0][0][rows], out[1][0][rows]], 1)
-        m = jnp.concatenate([out[0][1][rows], out[1][1][rows]], 1)
-        y = times_left(jnp.concatenate([m, r] if swap else [r, m], 0), w_ref, k)
+        y = times_left(split[i], w_ref, k)
         a, b = y[:h], y[h:]
         r, m = (b, a) if swap else (a, b)
         res_re[i] = [r[:, :h], r[:, h:]]
         res_im[i] = [m[:, :h], m[:, h:]]
+    yield
     return res_re, res_im
+
+
+def staggered(*runs):
+    live = list(enumerate(runs))
+    turn_of = 0
+    while live:
+        for item in list(live):
+            lag, run = item
+            if turn_of >= lag:
+                try:
+                    next(run)
+                except StopIteration:
+                    live.remove(item)
+        turn_of += 1
 
 
 PROP = (((0, False), (1, False)), ((0, True), (1, True)))
@@ -124,16 +148,7 @@
 
 def neighbours(rows, cols):
     r, c = place_of()
-    out = []
-    for dr, dc in AROUND:
-        ok = None
-        if dr:
-            ok = r > 0 if dr < 0 else r < rows - 1
-        if dc:
-            side = c > 0 if dc < 0 else c < cols - 1
-            ok = side if ok is None else jnp.logical_and(ok, side)
-        out.append((ok, (r + dr, c + dc)))
-    return out
+    return [(lax.rem(r + dr + rows, rows), lax.rem(c + dc + cols, cols)) for dr, dc in AROUND]
 
 
 def opposite(d):
@@ -147,45 +162,26 @@
     )
 
 
-def greet(around, extra):
-    barrier = pltpu.get_barrier_semaphore()
-    for ok, where in around:
-
-        @pl.when(ok)
-        def _(where=where):
-            pl.semaphore_signal(barrier, inc=1, device_id=where, device_id_type=MESH)
-
-    for where in extra:
-        pl.semaphore_signal(barrier, inc=1, device_id=where, device_id_type=MESH)
-
-
-def await_greetings(rows, cols, extra):
-    r, c = place_of()
-    tall = 1 + jnp.where(r > 0, 1, 0) + jnp.where(r < rows - 1, 1, 0)
-    wide = 1 + jnp.where(c > 0, 1, 0) + jnp.where(c < cols - 1, 1, 0)
-    pl.semaphore_wait(pltpu.get_barrier_semaphore(), tall * wide - 1 + len(extra))
-
-
-def swap_rims(around, sources, targets, send_sem, recv_sem, wave):
-    for d, (ok, where) in enumerate(around):
+def greet(peers):
+    for where in peers:
+        pl.semaphore_signal(pltpu.get_barrier_semaphore(), inc=1, device_id=where, device_id_type=MESH)
+
+
+CORNERS, STRAIGHT, ALONG, ACROSS = (4, 5, 6, 7), (0, 1, 2, 3), (0, 1), (2, 3)
+
+
+def swap_rims(around, sources, targets, send_sem, recv_sem, these):
+    for d in these:
         o = opposite(d)
-        copy = remote(sources[d], targets[o], send_sem.at[wave, d], recv_sem.at[wave, o], where)
-        pl.when(ok)(copy.start)
-        target = targets[d]
-
-        @pl.when(jnp.logical_not(ok))
-        def _(target=target):
-            target[...] = jnp.zeros(target.shape, target.dtype)
-
-
-def finish_rims(around, sources, targets, send_sem, recv_sem, wave):
-    for d, (ok, where) in enumerate(around):
-        copy = remote(sources[d], targets[d], send_sem.at[wave, d], recv_sem.at[wave, d], where)
-        pl.when(ok)(copy.wait)
+        remote(sources[d], targets[o], send_sem, recv_sem, around[d]).start()
 
 
 def both(ref, *at):
     return jnp.concatenate([ref[(*at, 0)], ref[(*at, 1)]], 1)
+
+
+def distant(count):
+    return sorted(range(count), key=lambda d: -min(d, count - d))
 
 
 def turn(x, lanes):
@@ -241,14 +237,19 @@
         k = lax.rem(z + d, nz)
         return lax.div(k, nzl) * CORES + 1 - core, lax.rem(k, nzl) * nxy + here
 
-    far = sorted(range(1, nz), key=lambda d: -min(d, nz - d))
+    far = distant(nz)[:-1]
+    spread = [oy * nx + ox for oy in distant(ny) for ox in distant(nx)][:-1]
 
     around = neighbours(rows, cols)
     extra = [partner]
     extra += [peer(d)[1] for d in range(1, nxy)]
     extra += [zpeer(d) for d in range(1, nz)]
     extra += [zother(d) for d in range(1, nz)]
-    greet(around, extra)
+    greet(around + extra)
+    above, below, before, after = r > 0, r < rows - 1, c > 0, c < cols - 1
+
+    def only(ok, value):
+        return jnp.where(ok, value, jnp.zeros_like(value))
 
     win = (win_a, win_b)
     inner = pl.ds(RIM, n)
@@ -276,7 +277,15 @@
             return win[l][k % 2, t, RIM + h * (k // 2) : RIM + h * (k // 2) + h, :]
 
         pl_buf[l], pr_buf[l] = pack_sides(lambda k: piece(1, k), lambda k: piece(2, k), quarter)
-    await_greetings(rows, cols, extra)
+    pl.semaphore_wait(pltpu.get_barrier_semaphore(), len(around) + len(extra))
+
+    def landed(ref, sem):
+        remote(ref, ref, sem, sem, partner).wait_recv()
+
+    def left(ref, sem):
+        remote(ref, ref, sem, sem, partner).wait_send()
+
+    wave = win[0].at[0, pl.ds(0, 2), :, :]
 
     ups, tops = pl.ds(0, RIM), pl.ds(RIM, RIM)
     lows, downs = pl.ds(n, RIM), pl.ds(n + RIM, RIM)
@@ -290,14 +299,13 @@
             ],
             [win[l].at[:, 1:3, ups, :], win[l].at[:, 1:3, downs, :], hl.at[l], hr.at[l]]
             + [hc.at[l, k] for k in range(4)],
-            send_halo,
-            recv_halo,
-            l,
+            send_halo.at[l],
+            recv_halo.at[l],
         )
         for l in (0, 1)
     ]
-    for l in (0, 1):
-        swap_rims(*halo[l])
+    swap_rims(*halo[0], CORNERS + STRAIGHT)
+    swap_rims(*halo[1], CORNERS + STRAIGHT)
 
     zeros = jnp.zeros((64, 128), jnp.float32)
     for p in range(npos):
@@ -325,33 +333,42 @@
         load.wait()
     offs = [(pos_ref[0, 0, p, 0], pos_ref[0, 0, p, 1]) for p in range(npos)]
     lane = lax.broadcasted_iota(jnp.int32, (RIM, 128), 1)
+    chunk = 2 * RIM
+    long_lane = lax.broadcasted_iota(jnp.int32, (chunk, 128), 1)
 
     def cut_slice(l):
-        finish_rims(*halo[l])
+        landed(wave, recv_halo.at[l])
+        left(wave, send_halo.at[l])
         for a in (0, 1):
+            for t in (1, 2):
+                win[l][a, t, 0:RIM, :] = only(above, win[l][a, t, 0:RIM, :])
+                win[l][a, t, RIM + n :, :] = only(below, win[l][a, t, RIM + n :, :])
             for k in (0, 1):
                 at = slice(RIM + h * k, RIM + h * k + h)
-                win[l][a, 0, at, :] = turn(hl[l], 96 - 32 * (2 * k + a))
-                win[l][a, 3, at, :] = turn(hr[l], -32 * (2 * k + a))
-            win[l][a, 0, 0:RIM, :] = turn(hc[l, 0], 96 - 32 * (2 + a))
-            win[l][a, 3, 0:RIM, :] = turn(hc[l, 1], -32 * (2 + a))
-            win[l][a, 0, RIM + n :, :] = turn(hc[l, 2], 96 - 32 * a)
-            win[l][a, 3, RIM + n :, :] = turn(hc[l, 3], -32 * a)
+                win[l][a, 0, at, :] = only(before, turn(hl[l], 96 - 32 * (2 * k + a)))
+                win[l][a, 3, at, :] = only(after, turn(hr[l], -32 * (2 * k + a)))
+            for k, (row, ok) in enumerate(((0, above), (RIM + n, below))):
+                lane_of = 32 * (2 * (1 - k) + a)
+                at = slice(row, row + RIM)
+                win[l][a, 0, at, :] = only(
+                    jnp.logical_and(ok, before), turn(hc[l, 2 * k], 96 - lane_of)
+                )
+                win[l][a, 3, at, :] = only(jnp.logical_and(ok, after), turn(hc[l, 2 * k + 1], -lane_of))
 
         def cut_rows(i, carry):
             for p in range(npos):
                 dy, dx = offs[p]
                 shift = lax.rem(128 - dx, 128)
-                high, low = lane >= 128 - dx, lane < -dx
+                high, low = long_lane >= 128 - dx, long_lane < -dx
                 for a in (0, 1):
-                    at = pl.ds(RIM + dy + i * RIM, RIM)
+                    at = pl.ds(RIM + dy + i * chunk, chunk)
                     t0, t1, t2, t3 = [pltpu.roll(win[l][a, t, at, :], shift, 1) for t in range(4)]
-                    to = rows_at(i * RIM, RIM)
+                    to = rows_at(i * chunk, chunk)
                     cut[p, 2 * l + a, 0, to, :] = jnp.where(high, t2, jnp.where(low, t0, t1))
                     cut[p, 2 * l + a, 1, to, :] = jnp.where(high, t3, jnp.where(low, t1, t2))
             return carry
 
-        lax.fori_loop(0, n // RIM, cut_rows, 0)
+        lax.fori_loop(0, n // chunk, cut_rows, 0)
 
     def keep(p, q, value):
         pad[p, q, 0, 64 : 64 + n, :] = value[:, :128]
@@ -388,6 +405,7 @@
 
     def place_slice(l):
         gcl[l], gcr[l] = place(l, (0, RIM + n))
+        swap_rims(*rims[l], CORNERS + ALONG)
 
         def go(i, carry):
             to = rows_at(i * RIM, RIM)
@@ -395,6 +413,7 @@
             return carry
 
         lax.fori_loop(0, h // RIM, go, 0)
+        swap_rims(*rims[l], ACROSS)
 
     rims = [
         (
@@ -402,41 +421,42 @@
             [grad.at[pl.ds(2 * l, 2), :, ups, :], grad.at[pl.ds(2 * l, 2), :, downs, :], gl.at[l], gr.at[l]]
             + [gcl.at[l], gcr.at[l]] * 2,
             [rt.at[l], rb.at[l], rl.at[l], rr.at[l]] + [corners.at[l, k] for k in range(4)],
-            send_rim,
-            recv_rim,
-            l,
+            send_rim.at[l],
+            recv_rim.at[l],
         )
         for l in (0, 1)
     ]
 
-    cut_slice(0)
-    for p in range(npos):
+    def first_pass(p):
         pr, pi = probe_ref[0], probe_ref[1]
         ar, ai = both(cut, p, 0), both(cut, p, 1)
-        re, im = sandwich(fold(pr * ar - pi * ai), fold(pr * ai + pi * ar), w_ref, *PROP)
+        re, im = yield from sandwich(
+            fold(pr * ar - pi * ai), fold(pr * ai + pi * ar), w_ref, *PROP
+        )
         mid[p, 0], mid[p, 1] = unfold(re), unfold(im)
-    cut_slice(1)
-    for p in range(npos):
+
+    def second_pass(p):
         qr, qi = mid[p, 0], mid[p, 1]
         br, bi = both(cut, p, 2), both(cut, p, 3)
-        re, im = sandwich(fold(qr * br - qi * bi), fold(qr * bi + qi * br), w_ref, *FORWARD)
+        re, im = yield from sandwich(
+            fold(qr * br - qi * bi), fold(qr * bi + qi * br), w_ref, *FORWARD
+        )
         for i in (0, 1):
             for j in (0, 1):
                 fr, fi = re[i][j], im[i][j]
                 seen_at = meas_ref[p, i * h : (i + 1) * h, j * h : (j + 1) * h]
                 ex = 2.0 * (fr * fr + fi * fi - seen_at)
                 re[i][j], im[i][j] = ex * fr, ex * fi
-        re, im = sandwich(re, im, w_ref, *BACKWARD)
+        re, im = yield from sandwich(re, im, w_ref, *BACKWARD)
         hr_, hi_ = unfold(re), unfold(im)
         qr, qi = mid[p, 0], mid[p, 1]
         keep(p, 2, qr * hr_ + qi * hi_)
         keep(p, 3, qr * hi_ - qi * hr_)
         br, bi = both(cut, p, 2), both(cut, p, 3)
         mid[p, 0], mid[p, 1] = br * hr_ + bi * hi_, br * hi_ - bi * hr_
-    place_slice(1)
-    swap_rims(*rims[1])
-    for p in range(npos):
-        re, im = sandwich(fold(mid[p, 0]), fold(mid[p, 1]), w_ref, *PROP_CONJ)
+
+    def third_pass(p):
+        re, im = yield from sandwich(fold(mid[p, 0]), fold(mid[p, 1]), w_ref, *PROP_CONJ)
         er, ei = unfold(re), unfold(im)
         pr, pi = probe_ref[0], probe_ref[1]
         keep(p, 0, pr * er + pi * ei)
@@ -449,6 +469,13 @@
             gp_ref[0] += ar * er + ai * ei
             gp_ref[1] += ar * ei - ai * er
 
+    cut_slice(0)
+    staggered(*[first_pass(p) for p in range(npos)])
+    cut_slice(1)
+    staggered(*[second_pass(p) for p in range(npos)])
+    place_slice(1)
+    staggered(*[third_pass(p) for p in range(npos)])
+
     def band(q):
         return rows_at(q * step, step)
 
@@ -459,27 +486,20 @@
         at = stripe(lax.rem(y + oy, ny))
         return at, remote(gp_ref.at[1 - core, at, :], theirs.at[at, :], send_pair, recv_pair.at[oy], partner)
 
-    for oy in reversed(range(ny)):
+    for oy in distant(ny):
         pair(oy)[1].start()
 
     place_slice(0)
-    swap_rims(*rims[0])
-
-    for oy in reversed(range(ny)):
+
+    for oy in distant(ny):
         at, copy = pair(oy)
         copy.wait_recv()
         ours[at, :] = gp_ref[core, at, :] + theirs[at, :]
-        for ox in reversed(range(nx)):
+        for ox in distant(nx):
             d = oy * nx + ox
             if d:
                 q, where = peer(d)
                 remote(ours.at[band(q), :], slots.at[d], send_xy, recv_xy, where).start()
-
-    def landed(ref, sem):
-        remote(ref, ref, sem, sem, partner).wait_recv()
-
-    def left(ref, sem):
-        remote(ref, ref, sem, sem, partner).wait_send()
 
     landed(slots.at[pl.ds(1, nxy - 1)], recv_xy)
     acc = ours[band(here), :]
@@ -490,7 +510,8 @@
     for d in far:
         remote(mine, zslots.at[z], send_z, recv_z, zpeer(d)).start()
 
-    first, final = lane < 32, lane >= 96
+    first_in = lane < jnp.where(before, 32, 0)
+    final_in = lane >= jnp.where(after, 96, 128)
     zero = jnp.zeros((RIM, 128), jnp.float32)
 
     def rows_of(l, k, i):
@@ -499,8 +520,8 @@
         for a in (0, 1):
             lane_of = 32 * (2 * k + a)
             ends = (
-                jnp.where(first, turn(rl[l, at, :], -lane_of), zero),
-                jnp.where(final, turn(rr[l, at, :], 96 - lane_of), zero),
+                jnp.where(first_in, turn(rl[l, at, :], -lane_of), zero),
+                jnp.where(final_in, turn(rr[l, at, :], 96 - lane_of), zero),
             )
             for t in (0, 1):
                 v = grad[2 * l + a, t, to, :] + ends[t]
@@ -510,18 +531,19 @@
         return functools.reduce(jnp.maximum, [best[8 * b : 8 * b + 8] for b in range(RIM // 8)])
 
     def add_edges(l):
-        for edge, (strip, to, c) in enumerate(((rt, RIM, 0), (rb, n, 2))):
+        for edge, (strip, to, ok) in enumerate(((rt, RIM, above), (rb, n, below))):
             for a in (0, 1):
                 lane_of = 32 * (2 * (1 - edge) + a)
                 sides = (
-                    jnp.where(first, turn(corners[l, c], -lane_of), zero),
-                    jnp.where(final, turn(corners[l, c + 1], 96 - lane_of), zero),
+                    jnp.where(first_in, turn(corners[l, 2 * edge], -lane_of), zero),
+                    jnp.where(final_in, turn(corners[l, 2 * edge + 1], 96 - lane_of), zero),
                 )
                 for t in (0, 1):
-                    grad[2 * l + a, t, to : to + RIM, :] += strip[l, a, t] + sides[t]
+                    grad[2 * l + a, t, to : to + RIM, :] += only(ok, strip[l, a, t] + sides[t])
 
     def finish_slice(l):
-        finish_rims(*rims[l])
+        landed(wave, recv_rim.at[l])
+        left(wave, send_rim.at[l])
         add_edges(l)
         peak = jnp.zeros((8, 128), jnp.float32)
         for k in (0, 1):
@@ -531,7 +553,7 @@
         return peak
 
     xpeak[0] = jnp.maximum(finish_slice(1), finish_slice(0))
-    for d in reversed(range(1, nxy)):
+    for d in spread:
         remote(xpeak.at[0], xpeak.at[d], send_xm, recv_xm, peer(d)[1]).start()
 
     landed(zslots.at[pl.ds(0, nz - 1)], recv_z)
@@ -540,7 +562,7 @@
         acc = acc + zslots[k]
     total_ref[pl.ds(core, 1), band(here), :] = acc[None]
     block = total_ref.at[core, band(here), :]
-    for d in reversed(range(1, nxy)):
+    for d in spread:
         remote(block, block, send_all, recv_all.at[d // nx], peer(d)[1]).start()
 
     landed(xpeak.at[pl.ds(1, nxy - 1)], recv_xm)
@@ -560,7 +582,7 @@
         landed(total_ref.at[core, pl.ds(0, count * step), :], recv_all.at[oy])
         remote(block, block, send_back, recv_back, partner).start()
 
-    for oy in range(ny):
+    for oy in reversed(distant(ny)):
         forward(oy)
     landed(zpeak.at[pl.ds(1, 2 * nz - 1)], recv_zm)
     peak = zpeak[0]
@@ -614,7 +636,7 @@
     ]
     scratch = [pltpu.SMEM(positions.shape, jnp.int32)]
     scratch += [VMEM(shape, jnp.bfloat16 if i in (2, 3) else f32) for i, shape in enumerate(buffers)]
-    scratch += [dma((9,)), dma((2, 8)), dma((2, 8)), dma((2, 8)), dma((2, 8))]
+    scratch += [dma((9,)), dma((2,)), dma((2,)), dma((2,)), dma((2,))]
     scratch += [dma, dma((nyx[0],)), dma, dma, dma, dma]
     scratch += [dma] * 4 + [dma, dma((nyx[0],)), dma, dma]
     object_out, probe_out = pl.pallas_call(

time: 54.4 us -> 51.7 us (0.950)
  Pallas kernels: 51.9 us -> 49.2 us
    pallas_call x1, Pallas kernels: 51.9 us -> 49.2 us  [local(): pl.pallas_call(functools.partial(kernel, rows, cols, nyx), out_shape=(jax...]
where the time goes in v5:
time: 51.7 us; the launch traced here: 51.6 us
  Pallas kernels  49.2 us (95%)
  local copies, waits for them, and re-layouts  1.77 us (3%)
  between operations  0.64 us (1%)
    pallas_call x1, Pallas kernels, local(): pl.pallas_call(functools.partial(kernel, rows, cols, nyx), out_shape=(jax...  49.2 us
    unnamed x2, local copies, waits for them, and re-layouts  1.77 us

profile of v5, /device:TPU:1, one launch (start us, length us, event | category | flops | bytes accessed | tf_op | source)
XLA Modules:
  0.0 51.6 jit_solution(1768515004437103712)
XLA Ops:
  0.6 49.2 %step.1 = (f32[4,256,256]{2,1,0:T(8,128)S(1)}, f32[2,256,256]{2,1,0:T(8,128)S(1)}) custom-call(s32[1,1,2,2]{3,2,1,0:T(2,128)} %pos_in.1, f32[4,256,256]{2,1,0:T(8,128)} %bitcast.4, f32[2,256,256]{2,1,0:T(8,128)} %probe_in.1, f32[2,256,256]{2,1,0:T(8,128)} %bitcast.5, bf16[5,2,256,256]{3,2,1,0:T(8,128)(2,1)} %constant.4.clone.table_in, ...), custom_call_target="tpu_custom_call" | custom-call | tf_op jit(solution)/shard_map/step/pallas_call | solution.py:642
  49.8 1.0 %copy.10 = f32[2,2,256,256]{3,2,1,0:T(8,128)} copy(f32[2,2,256,256]{3,2,1,0:T(8,128)S(1)} %bitcast.3) | data formatting | bytes 2097152
  50.8 0.8 %copy.11 = f32[2,256,256]{2,1,0:T(8,128)} copy(f32[2,256,256]{2,1,0:T(8,128)S(1)} %get-tuple-element.9) | data formatting | bytes 1048576

commit v6 on v5

--- a/solution.py
+++ b/solution.py
@@ -59,13 +59,17 @@
 def times_right(split, w_ref, k):
     high, low = split
     wh, wl = w_ref[k, 0], w_ref[k, 1]
-    return dot(jnp.concatenate([high, low, high], 1), jnp.concatenate([wh, wh, wl], 0))
+    rows = high.shape[0]
+    y = dot(jnp.concatenate([high, low], 0), wh)
+    return y[:rows] + (y[rows:] + dot(high, wl))
 
 
 def times_left(split, w_ref, k):
     high, low = split
     wh, wl = w_ref[k, 0], w_ref[k, 1]
-    return dot(jnp.concatenate([wh, wh, wl], 1), jnp.concatenate([high, low, high], 0))
+    rows = wh.shape[0]
+    y = dot(jnp.concatenate([wh, wl], 0), high)
+    return y[:rows] + (y[rows:] + dot(wh, low))
 
 
 def fold(x):
@@ -139,6 +143,8 @@
 
 
 def rows_at(start, size):
+    if isinstance(start, int):
+        return pl.ds(start, size)
     return pl.ds(pl.multiple_of(start, size), size)
 
 
@@ -238,14 +244,14 @@
         return lax.div(k, nzl) * CORES + 1 - core, lax.rem(k, nzl) * nxy + here
 
     far = distant(nz)[:-1]
-    spread = [oy * nx + ox for oy in distant(ny) for ox in distant(nx)][:-1]
+    spread = sorted(range(1, nxy), key=lambda d: -min(d // nx, ny - d // nx) - min(d % nx, nx - d % nx))
 
     around = neighbours(rows, cols)
     extra = [partner]
     extra += [peer(d)[1] for d in range(1, nxy)]
     extra += [zpeer(d) for d in range(1, nz)]
     extra += [zother(d) for d in range(1, nz)]
-    greet(around + extra)
+    greet(extra[::-1] + around)
     above, below, before, after = r > 0, r < rows - 1, c > 0, c < cols - 1
 
     def only(ok, value):
@@ -403,6 +409,15 @@
         right, left = pack_sides(lambda k: got[k][3], lambda k: got[k][0], quarter)
         return left, right
 
+    def place_steps(l):
+        gcl[l], gcr[l] = place(l, (0, RIM + n))
+        swap_rims(*rims[l], CORNERS + ALONG)
+        for i in range(h // RIM):
+            yield
+            to = pl.ds(i * RIM, RIM)
+            gl[l, to, :], gr[l, to, :] = place(l, (i * RIM + RIM, i * RIM + RIM + h))
+        swap_rims(*rims[l], ACROSS)
+
     def place_slice(l):
         gcl[l], gcr[l] = place(l, (0, RIM + n))
         swap_rims(*rims[l], CORNERS + ALONG)
@@ -473,8 +488,7 @@
     staggered(*[first_pass(p) for p in range(npos)])
     cut_slice(1)
     staggered(*[second_pass(p) for p in range(npos)])
-    place_slice(1)
-    staggered(*[third_pass(p) for p in range(npos)])
+    staggered(*[third_pass(p) for p in range(npos)], place_steps(1))
 
     def band(q):
         return rows_at(q * step, step)
@@ -548,7 +562,7 @@
         peak = jnp.zeros((8, 128), jnp.float32)
         for k in (0, 1):
             peak = lax.fori_loop(
-                0, h // RIM, lambda i, m, k=k: jnp.maximum(m, rows_of(l, k, i)), peak
+                0, h // RIM, lambda i, m, k=k: jnp.maximum(m, rows_of(l, k, i)), peak, unroll=True
             )
         return peak
 
@@ -563,8 +577,11 @@
     total_ref[pl.ds(core, 1), band(here), :] = acc[None]
     block = total_ref.at[core, band(here), :]
     for d in spread:
-        remote(block, block, send_all, recv_all.at[d // nx], peer(d)[1]).start()
-
+        remote(block, block, send_all, recv_all.at[d], peer(d)[1]).start()
+
+    nearest = [0] + spread[::-1]
+    forward_own = remote(block, block, send_back, recv_back, partner)
+    forward_own.start()
     landed(xpeak.at[pl.ds(1, nxy - 1)], recv_xm)
     peak = xpeak[0]
     for d in range(1, nxy):
@@ -575,15 +592,14 @@
         remote(zpeak.at[0], zpeak.at[nz + d], send_zm, recv_zm, zother(d)).start()
     remote(zpeak.at[0], zpeak.at[nz], send_zm, recv_zm, partner).start()
 
-    def forward(oy):
-        at = stripe(lax.rem(y + ny - oy, ny))
-        block = total_ref.at[core, at, :]
-        count = nx - 1 if oy == 0 else nx
-        landed(total_ref.at[core, pl.ds(0, count * step), :], recv_all.at[oy])
+    def forward(d):
+        q = lax.rem(y + ny - d // nx, ny) * nx + lax.rem(x + nx - d % nx, nx)
+        block = total_ref.at[core, band(q), :]
+        landed(block, recv_all.at[d])
         remote(block, block, send_back, recv_back, partner).start()
 
-    for oy in reversed(distant(ny)):
-        forward(oy)
+    for d in nearest[1:]:
+        forward(d)
     landed(zpeak.at[pl.ds(1, 2 * nz - 1)], recv_zm)
     peak = zpeak[0]
     for d in range(1, 2 * nz):
@@ -601,7 +617,7 @@
                 )
         return carry
 
-    lax.fori_loop(0, n // RIM, next_rows, 0)
+    lax.fori_loop(0, n // RIM, next_rows, 0, unroll=2)
     landed(total_ref.at[core], recv_back)
     probe_out[...] = probe_ref[...] - (2.0 / (rows * cols)) * total_ref[...]
     left(total_ref.at[core], send_back)
@@ -611,6 +627,16 @@
     left(zslots.at[pl.ds(0, nz - 1)], send_z)
     left(zpeak.at[pl.ds(1, 2 * nz - 1)], send_zm)
     left(xpeak.at[pl.ds(1, nxy - 1)], send_xm)
+
+
+def hand_out(object_ref, probe_ref, object_out, probe_out, sem):
+    copies = [(object_ref.at[q], object_out.at[q]) for q in range(4)]
+    copies += [(probe_ref.at[q], probe_out.at[q]) for q in range(2)]
+    copies = [pltpu.make_async_copy(a, b, sem.at[i]) for i, (a, b) in enumerate(copies)]
+    for copy in copies:
+        copy.start()
+    for copy in copies:
+        copy.wait()
 
 
 def local(rows, cols, nyx, table, perm, object_in, probe_in, positions, intensity):
@@ -638,7 +664,7 @@
     scratch += [VMEM(shape, jnp.bfloat16 if i in (2, 3) else f32) for i, shape in enumerate(buffers)]
     scratch += [dma((9,)), dma((2,)), dma((2,)), dma((2,)), dma((2,))]
     scratch += [dma, dma((nyx[0],)), dma, dma, dma, dma]
-    scratch += [dma] * 4 + [dma, dma((nyx[0],)), dma, dma]
+    scratch += [dma] * 4 + [dma, dma((nxy,)), dma, dma]
     object_out, probe_out = pl.pallas_call(
         functools.partial(kernel, rows, cols, nyx),
         out_shape=(jax.ShapeDtypeStruct((4, n, n), f32), jax.ShapeDtypeStruct((2, n, n), f32)),
@@ -658,6 +684,15 @@
             )
         )
     )
+    object_out, probe_out = pl.pallas_call(
+        hand_out,
+        out_shape=(jax.ShapeDtypeStruct((4, n, n), f32), jax.ShapeDtypeStruct((2, n, n), f32)),
+        in_specs=[vmem, vmem],
+        out_specs=(hbm, hbm),
+        scratch_shapes=[dma((6,))],
+        compiler_params=pltpu.CompilerParams(vmem_limit_bytes=2**20),
+        name="hand_out",
+    )(object_out, probe_out)
     return object_out.reshape(object_in.shape), probe_out
 
 

time: 51.7 us -> 50 us (0.967)
  local copies, waits for them, and re-layouts: 1.77 us -> 0 us
    unnamed x2 -> x0, local copies, waits for them, and re-layouts: 1.77 us -> none
    pallas_call x0 -> x1, Pallas kernels: none -> 1.19 us  [local(): pl.pallas_call(hand_out, out_shape=(jax.ShapeDtypeStruct((4, n, n), f32),...]
    pallas_call x1, Pallas kernels: 49.2 us -> 48.1 us  [local(): pl.pallas_call(functools.partial(kernel, rows, cols, nyx), out_shape=(jax...]
where the time goes in v6:
time: 50 us; the launch traced here: 49.9 us
  Pallas kernels  49.3 us (99%)
  between operations  0.64 us (1%)
    pallas_call x1, Pallas kernels, local(): pl.pallas_call(functools.partial(kernel, rows, cols, nyx), out_shape=(jax...  48.1 us
    pallas_call x1, Pallas kernels, local(): pl.pallas_call(hand_out, out_shape=(jax.ShapeDtypeStruct((4, n, n), f32),...  1.19 us

profile of v6, /device:TPU:1, one launch (start us, length us, event | category | flops | bytes accessed | tf_op | source)
XLA Modules:
  0.0 49.9 jit_solution(13352975888230704043)
XLA Ops:
  0.6 48.1 %step.1 = (f32[4,256,256]{2,1,0:T(8,128)S(1)}, f32[2,256,256]{2,1,0:T(8,128)S(1)}) custom-call(s32[1,1,2,2]{3,2,1,0:T(2,128)} %pos_in.1, f32[4,256,256]{2,1,0:T(8,128)} %bitcast.3, f32[2,256,256]{2,1,0:T(8,128)} %probe_in.1, f32[2,256,256]{2,1,0:T(8,128)} %bitcast.4, bf16[5,2,256,256]{3,2,1,0:T(8,128)(2,1)} %constant.4.clone.table_in, ...), custom_call_target="tpu_custom_call" | custom-call | tf_op jit(solution)/shard_map/step/pallas_call | solution.py:668
  48.7 1.2 %hand_out.1 = (f32[4,256,256]{2,1,0:T(8,128)}, f32[2,256,256]{2,1,0:T(8,128)}) custom-call(f32[4,256,256]{2,1,0:T(8,128)S(1)} %get-tuple-element.6.object_ref, f32[2,256,256]{2,1,0:T(8,128)S(1)} %get-tuple-element.7.probe_ref), custom_call_target="tpu_custom_call" | custom-call | tf_op jit(solution)/shard_map/hand_out/pallas_call | solution.py:687

commit v7 on v6

--- a/solution.py
+++ b/solution.py
@@ -374,7 +374,7 @@
                     cut[p, 2 * l + a, 1, to, :] = jnp.where(high, t3, jnp.where(low, t1, t2))
             return carry
 
-        lax.fori_loop(0, n // chunk, cut_rows, 0)
+        lax.fori_loop(0, n // chunk, cut_rows, 0, unroll=True)
 
     def keep(p, q, value):
         pad[p, q, 0, 64 : 64 + n, :] = value[:, :128]
@@ -418,18 +418,6 @@
             gl[l, to, :], gr[l, to, :] = place(l, (i * RIM + RIM, i * RIM + RIM + h))
         swap_rims(*rims[l], ACROSS)
 
-    def place_slice(l):
-        gcl[l], gcr[l] = place(l, (0, RIM + n))
-        swap_rims(*rims[l], CORNERS + ALONG)
-
-        def go(i, carry):
-            to = rows_at(i * RIM, RIM)
-            gl[l, to, :], gr[l, to, :] = place(l, (i * RIM + RIM, i * RIM + RIM + h))
-            return carry
-
-        lax.fori_loop(0, h // RIM, go, 0)
-        swap_rims(*rims[l], ACROSS)
-
     rims = [
         (
             around,
@@ -503,7 +491,7 @@
     for oy in distant(ny):
         pair(oy)[1].start()
 
-    place_slice(0)
+    staggered(place_steps(0))
 
     for oy in distant(ny):
         at, copy = pair(oy)

time: 50 us -> 49.8 us (level)
  no operation moved by 1% of the time
where the time goes in v7:
time: 49.8 us; the launch traced here: 50 us
  Pallas kernels  49.3 us (99%)
  between operations  0.64 us (1%)
    pallas_call x1, Pallas kernels, local(): pl.pallas_call(functools.partial(kernel, rows, cols, nyx), out_shape=(jax...  48.1 us
    pallas_call x1, Pallas kernels, local(): pl.pallas_call(hand_out, out_shape=(jax.ShapeDtypeStruct((4, n, n), f32),...  1.19 us

profile of v7, /device:TPU:1, one launch (start us, length us, event | category | flops | bytes accessed | tf_op | source)
XLA Modules:
  0.0 50.0 jit_solution(11875972919012115688)
XLA Ops:
  0.6 48.1 %step.1 = (f32[4,256,256]{2,1,0:T(8,128)S(1)}, f32[2,256,256]{2,1,0:T(8,128)S(1)}) custom-call(s32[1,1,2,2]{3,2,1,0:T(2,128)} %pos_in.1, f32[4,256,256]{2,1,0:T(8,128)} %bitcast.3, f32[2,256,256]{2,1,0:T(8,128)} %probe_in.1, f32[2,256,256]{2,1,0:T(8,128)} %bitcast.4, bf16[5,2,256,256]{3,2,1,0:T(8,128)(2,1)} %constant.4.clone.table_in, ...), custom_call_target="tpu_custom_call" | custom-call | tf_op jit(solution)/shard_map/step/pallas_call | solution.py:656
  48.8 1.2 %hand_out.1 = (f32[4,256,256]{2,1,0:T(8,128)}, f32[2,256,256]{2,1,0:T(8,128)}) custom-call(f32[4,256,256]{2,1,0:T(8,128)S(1)} %get-tuple-element.6.object_ref, f32[2,256,256]{2,1,0:T(8,128)S(1)} %get-tuple-element.7.probe_ref), custom_call_target="tpu_custom_call" | custom-call | tf_op jit(solution)/shard_map/hand_out/pallas_call | solution.py:675

commit v8 on v7

--- a/solution.py
+++ b/solution.py
@@ -503,15 +503,6 @@
                 q, where = peer(d)
                 remote(ours.at[band(q), :], slots.at[d], send_xy, recv_xy, where).start()
 
-    landed(slots.at[pl.ds(1, nxy - 1)], recv_xy)
-    acc = ours[band(here), :]
-    for d in range(1, nxy):
-        acc = acc + slots[d]
-    mine[...] = acc
-    zslots[pl.ds(z, 1)] = acc[None]
-    for d in far:
-        remote(mine, zslots.at[z], send_z, recv_z, zpeer(d)).start()
-
     first_in = lane < jnp.where(before, 32, 0)
     final_in = lane >= jnp.where(after, 96, 128)
     zero = jnp.zeros((RIM, 128), jnp.float32)
@@ -554,7 +545,18 @@
             )
         return peak
 
-    xpeak[0] = jnp.maximum(finish_slice(1), finish_slice(0))
+    early = finish_slice(1)
+
+    landed(slots.at[pl.ds(1, nxy - 1)], recv_xy)
+    acc = ours[band(here), :]
+    for d in range(1, nxy):
+        acc = acc + slots[d]
+    mine[...] = acc
+    zslots[pl.ds(z, 1)] = acc[None]
+    for d in far:
+        remote(mine, zslots.at[z], send_z, recv_z, zpeer(d)).start()
+
+    xpeak[0] = jnp.maximum(early, finish_slice(0))
     for d in spread:
         remote(xpeak.at[0], xpeak.at[d], send_xm, recv_xm, peer(d)[1]).start()
 

time: 49.8 us -> 49.8 us (level)
  no operation moved by 1% of the time
where the time goes in v8:
time: 49.8 us; the launch traced here: 49.7 us
  Pallas kernels  49.1 us (99%)
  between operations  0.64 us (1%)
    pallas_call x1, Pallas kernels, local(): pl.pallas_call(functools.partial(kernel, rows, cols, nyx), out_shape=(jax...  47.9 us
    pallas_call x1, Pallas kernels, local(): pl.pallas_call(hand_out, out_shape=(jax.ShapeDtypeStruct((4, n, n), f32),...  1.19 us

profile of v8, /device:TPU:1, one launch (start us, length us, event | category | flops | bytes accessed | tf_op | source)
XLA Modules:
  0.0 49.7 jit_solution(8680730093299747858)
XLA Ops:
  0.6 47.9 %step.1 = (f32[4,256,256]{2,1,0:T(8,128)S(1)}, f32[2,256,256]{2,1,0:T(8,128)S(1)}) custom-call(s32[1,1,2,2]{3,2,1,0:T(2,128)} %pos_in.1, f32[4,256,256]{2,1,0:T(8,128)} %bitcast.3, f32[2,256,256]{2,1,0:T(8,128)} %probe_in.1, f32[2,256,256]{2,1,0:T(8,128)} %bitcast.4, bf16[5,2,256,256]{3,2,1,0:T(8,128)(2,1)} %constant.4.clone.table_in, ...), custom_call_target="tpu_custom_call" | custom-call | tf_op jit(solution)/shard_map/step/pallas_call | solution.py:658
  48.6 1.2 %hand_out.1 = (f32[4,256,256]{2,1,0:T(8,128)}, f32[2,256,256]{2,1,0:T(8,128)}) custom-call(f32[4,256,256]{2,1,0:T(8,128)S(1)} %get-tuple-element.6.object_ref, f32[2,256,256]{2,1,0:T(8,128)S(1)} %get-tuple-element.7.probe_ref), custom_call_target="tpu_custom_call" | custom-call | tf_op jit(solution)/shard_map/hand_out/pallas_call | solution.py:677
